TPU v7x, 512 devices: a whole 4x8x8 slice. The times are simulated.
512 devices in a mesh: ax: 8 (over y), circ: 16 (over z, core), gap: 4 (over x).
Axes of the slice: x: 4, y: 8, z: 8, core: 2. Of those that a mesh axis runs over, the one named last changes fastest.
Arguments:
- w_old: float32 [64, 512, 512], P('ax', 'circ', 'gap'), may hold values from -3 to 3
- yield_stress: float32 [64, 512, 512], P('ax', 'circ', 'gap'), may hold values from 1 to 10
- force: float32 [64, 512, 512], P('ax', 'circ', 'gap'), may hold values from -9 to 9
- part_xi: float32 [8, 16, 4, 3, 8192], P('ax', 'circ', 'gap'), may hold values from -1 to 1
- part_vel: float32 [8, 16, 4, 3, 8192], P('ax', 'circ', 'gap'), may hold values from -3 to 3
- part_moment: float32 [8, 16, 4, 3, 8192], P('ax', 'circ', 'gap'), may hold values from -4 to 4
- elements: int32 [8, 16, 4, 8192], P('ax', 'circ', 'gap'), may hold values from 0 to 63
- new_elements: int32 [8, 16, 4, 8192], P('ax', 'circ', 'gap'), may hold values from 0 to 63
- send_slots: int32 [8, 16, 4, 6, 1024], P('ax', 'circ', 'gap'), may hold values from 0 to 8191, as said below
- counts: int32 [8, 16, 4, 6], P('ax', 'circ', 'gap'), may hold values from 1 to 1024, as said below
Outputs:
- w_new: float32 [64, 512, 512], P('ax', 'circ', 'gap')
- kept: float32 [8, 16, 4, 9, 8192], P('ax', 'circ', 'gap')
- arrived: float32 [8, 16, 4, 6, 9, 1024], P('ax', 'circ', 'gap')
Inputs may be any that keep to these rules, and one draw needn't show every extreme that they name: `send_slots`: on each device the 6144 entries are distinct particle indices. `counts`: on every device one direction has exactly 1024 live slots.
All inputs are finite; a program needn't handle non-finite values.
Results may differ from a plain program's by a relative error of at most 0.0003.
Values sent between devices are 32-bit elements; how exact they have to be, the bound alone decides.
A program may use at most 64 MiB of HBM per device.

v0:
```python
import math

import jax
import jax.numpy as jnp
import numpy as np
from jax import lax
from jax.sharding import PartitionSpec as P

ITERS = 3


GLL_NODES = np.array(
    [
        -1.0,
        -0.8717401485096066,
        -0.5917001814331423,
        -0.2092992179024789,
        0.2092992179024789,
        0.5917001814331423,
        0.8717401485096066,
        1.0,
    ]
)
GLL_WEIGHTS = np.array(
    [
        0.03571428571428571,
        0.2107042271435061,
        0.3411226924835044,
        0.4124587946587038,
        0.4124587946587038,
        0.3411226924835044,
        0.2107042271435061,
        0.03571428571428571,
    ]
)
TIME_STEP = 0.25
PLASTIC_VISC = 0.05
REGULAR_SHIFT = 1.0
DRAG_RELAX = 0.4
METRIC = (1.0, 1.0, 4.0)
JACOBIAN = 0.25


def with_halo(value, sides, width):
    for axis, dim in sides:
        size, length = (lax.axis_size(axis), value.shape[dim])
        up = [(i, (i + 1) % size) for i in range(size)]
        down = [(j, i) for i, j in up]
        last = lax.slice_in_dim(value, length - width, length, axis=dim)
        first = lax.slice_in_dim(value, 0, width, axis=dim)
        before = lax.ppermute(last, axis, up)
        after = lax.ppermute(first, axis, down)
        value = jnp.concatenate([before, value, after], axis=dim)
    return value


def from_behind(block, axis, distance):
    devices = range(lax.axis_size(axis))
    route = [(i - distance, i) for i in devices if i - distance in devices]
    return lax.ppermute(block, axis, route)


def passed_along(value, axis, by):
    length = lax.axis_size(axis)
    return lax.ppermute(value, axis, [(i, (i + by) % length) for i in range(length)])


def bary_weights():
    identity_mask = np.eye(8, dtype=bool)
    differences = np.where(identity_mask, 1.0, GLL_NODES[:, None] - GLL_NODES[None, :])
    return (1.0 / np.prod(differences, axis=1), differences)


def diff_table():
    barycentric, differences = bary_weights()
    identity_mask = np.eye(8, dtype=bool)
    off_diag = np.where(
        identity_mask, 0.0, barycentric[None, :] / barycentric[:, None] / differences
    )
    diff_matrix = off_diag - np.eye(8) * np.sum(off_diag, axis=1)[:, None]
    return diff_matrix.astype(np.float32)


def lagrange_basis(points):
    barycentric, unused = bary_weights()
    columns = []
    for column in range(8):
        product_term = jnp.full(points.shape, np.float32(barycentric[column]), points.dtype)
        for other_node in range(8):
            if other_node != column:
                product_term = product_term * (points - np.float32(GLL_NODES[other_node]))
        columns.append(product_term)
    return jnp.stack(columns)


def sample_elements(element_table, element_ids, points):
    basis_first = lagrange_basis(points[0])
    basis_second = lagrange_basis(points[1])
    basis_third = lagrange_basis(points[2])
    combined = (
        basis_first[:, None, None, :]
        * basis_second[None, :, None, :]
        * basis_third[None, None, :, :]
    )
    combined = combined.reshape(512, points.shape[1])
    picked = jnp.take(element_table, element_ids, axis=1)
    return jnp.sum(picked * combined, axis=0)


def sample_blocks(element_table, element_ids, points):
    total_rows = element_ids.shape[0]
    block_len = math.gcd(total_rows, 2048)
    pieces = total_rows // block_len

    def one_block(block_items):
        return sample_elements(element_table, block_items[0], block_items[1])

    grouped_points = jnp.transpose(points.reshape(3, pieces, block_len), (1, 0, 2))
    sampled = lax.map(one_block, (element_ids.reshape(pieces, block_len), grouped_points))
    return sampled.reshape(total_rows)


def advance(state, fluid):
    axial_vel = state[3] + DRAG_RELAX * (fluid - state[3])
    circ_vel = state[4] * (1.0 - DRAG_RELAX)
    radial_vel = state[5] * (1.0 - DRAG_RELAX)
    return jnp.stack(
        [
            state[0] + TIME_STEP * METRIC[0] * axial_vel,
            state[1] + TIME_STEP * METRIC[1] * circ_vel,
            state[2] + TIME_STEP * METRIC[2] * radial_vel,
            axial_vel,
            circ_vel,
            radial_vel,
            state[6],
            state[7],
            state[8],
        ]
    )


def pack_leaving(state, new_ids, slots, live_counts):
    flat_slots = slots.reshape(-1)
    capacity = slots.shape[1]
    chosen = jnp.transpose(jnp.take(state, flat_slots, axis=1).reshape(9, 6, capacity), (1, 0, 2))
    targets = jnp.take(new_ids, flat_slots).reshape(6, 1, capacity).astype(state.dtype)
    live_flag = (jnp.arange(capacity)[None, :] < live_counts[:, None]).astype(state.dtype)
    buffers = (
        jnp.concatenate([chosen, targets, jnp.ones_like(targets)], axis=1) * live_flag[:, None, :]
    )
    departed = jnp.zeros((state.shape[1],), state.dtype).at[flat_slots].max(live_flag.reshape(-1))
    return (buffers, departed)


def settle_arrivals(arrivals, element_table):
    capacity = arrivals.shape[2]
    flattened = jnp.transpose(arrivals, (1, 0, 2)).reshape(11, 6 * capacity)
    element_ids = flattened[9].astype(jnp.int32)
    fluid = sample_blocks(element_table, element_ids, flattened[0:3])
    moved = advance(flattened[0:9], fluid) * flattened[10][None, :]
    return jnp.transpose(moved.reshape(9, 6, capacity), (1, 0, 2))


def face_share(local_count, position, parts, open_ends):
    node_ids = jnp.arange(local_count) + position * local_count
    local_point = node_ids % 8
    on_face = (local_point == 0) | (local_point == 7)
    if open_ends:
        on_face = on_face & (node_ids != 0) & (node_ids != local_count * parts - 1)
    return jnp.where(on_face, 0.5, 1.0).astype(jnp.float32)


def wall_mask(local_count, position, parts):
    node_ids = jnp.arange(local_count) + position * local_count
    return jnp.where((node_ids == 0) | (node_ids == local_count * parts - 1), 0.0, 1.0).astype(
        jnp.float32
    )


def quad_weights(count_first, count_second, count_third):
    first_w = jnp.asarray(np.tile(GLL_WEIGHTS, count_first // 8).astype(np.float32))
    second_w = jnp.asarray(np.tile(GLL_WEIGHTS, count_second // 8).astype(np.float32))
    third_w = jnp.asarray(np.tile(GLL_WEIGHTS, count_third // 8).astype(np.float32))
    return first_w[:, None, None] * second_w[None, :, None] * third_w[None, None, :]


def local_derive(nodal_field, diff_matrix, axis_pos, transposed):
    base_matrix = diff_matrix.T if transposed else diff_matrix
    matrix = jnp.asarray(
        np.kron(np.eye(nodal_field.shape[axis_pos] // 8, dtype=np.float32), base_matrix)
    )
    patterns = ("ij,jkl->ikl", "ij,kjl->kil", "ij,klj->kli")
    return jnp.einsum(patterns[axis_pos], matrix, nodal_field, precision=lax.Precision.HIGHEST)


def along(axis_pos, piece):
    selector = [slice(None), slice(None), slice(None)]
    selector[axis_pos] = piece
    return tuple(selector)


def fold_faces(padded, axis_pos):
    length = padded.shape[axis_pos] - 2
    inner_part = lax.slice_in_dim(padded, 1, length + 1, axis=axis_pos)
    firsts = inner_part[along(axis_pos, slice(0, None, 8))]
    lasts = inner_part[along(axis_pos, slice(7, None, 8))]
    before = jnp.concatenate(
        [padded[along(axis_pos, slice(0, 1))], lasts[along(axis_pos, slice(0, -1))]], axis=axis_pos
    )
    after = jnp.concatenate(
        [
            firsts[along(axis_pos, slice(1, None))],
            padded[along(axis_pos, slice(length + 1, length + 2))],
        ],
        axis=axis_pos,
    )
    return (
        inner_part.at[along(axis_pos, slice(0, None, 8))]
        .add(before)
        .at[along(axis_pos, slice(7, None, 8))]
        .add(after)
    )


def edge_gate(local_count, position, last_index):
    gate_values = jnp.ones((local_count + 2,), jnp.float32)
    gate_values = gate_values.at[0].set(jnp.where(position == 0, 0.0, 1.0))
    return gate_values.at[local_count + 1].set(jnp.where(position == last_index, 0.0, 1.0))


def assemble(nodal_field):
    padded = with_halo(nodal_field, (("ax", 0), ("circ", 1), ("gap", 2)), 1)
    ax_gate = edge_gate(nodal_field.shape[0], lax.axis_index("ax"), lax.axis_size("ax") - 1)
    gap_gate = edge_gate(nodal_field.shape[2], lax.axis_index("gap"), lax.axis_size("gap") - 1)
    padded = padded * ax_gate[:, None, None] * gap_gate[None, None, :]
    folded = fold_faces(padded, 0)
    folded = fold_faces(folded, 1)
    return fold_faces(folded, 2)


def migrate_each(buffers):
    from_ax_low = from_behind(buffers[0], "ax", 1)
    from_ax_high = from_behind(buffers[1], "ax", -1)
    from_circ_low = passed_along(buffers[2], "circ", 1)
    from_circ_high = passed_along(buffers[3], "circ", -1)
    from_gap_low = from_behind(buffers[4], "gap", 1)
    from_gap_high = from_behind(buffers[5], "gap", -1)
    return jnp.stack(
        [from_ax_low, from_ax_high, from_circ_low, from_circ_high, from_gap_low, from_gap_high]
    )


def element_table_of(nodal_field):
    extent = nodal_field.shape
    element_grid = nodal_field.reshape(extent[0] // 8, 8, extent[1] // 8, 8, extent[2] // 8, 8)
    return jnp.transpose(element_grid, (1, 3, 5, 0, 2, 4)).reshape(512, -1)


def shards(
    w_old,
    yield_stress,
    force,
    part_xi,
    part_vel,
    part_moment,
    elements,
    new_elements,
    send_slots,
    counts,
):
    state = jnp.concatenate([part_xi[0, 0, 0], part_vel[0, 0, 0], part_moment[0, 0, 0]], axis=0)
    buffers, departed = pack_leaving(
        state, new_elements[0, 0, 0], send_slots[0, 0, 0], counts[0, 0, 0]
    )
    arrivals = migrate_each(buffers)
    diff_matrix = diff_table()
    extent = w_old.shape
    quadrature = quad_weights(extent[0], extent[1], extent[2])
    node_share = (
        face_share(extent[0], lax.axis_index("ax"), lax.axis_size("ax"), True)[:, None, None]
        * face_share(extent[1], lax.axis_index("circ"), lax.axis_size("circ"), False)[None, :, None]
        * face_share(extent[2], lax.axis_index("gap"), lax.axis_size("gap"), True)[None, None, :]
    )
    wall_gate = wall_mask(extent[2], lax.axis_index("gap"), lax.axis_size("gap"))[None, None, :]
    squares = REGULAR_SHIFT**2
    for axis_pos in range(3):
        gradient = local_derive(w_old, diff_matrix, axis_pos, False) * METRIC[axis_pos]
        squares = squares + gradient * gradient
    viscosity = PLASTIC_VISC + yield_stress / jnp.sqrt(squares)
    weighted = quadrature * viscosity
    stiffness = [weighted * (JACOBIAN * METRIC[axis_pos] ** 2) for axis_pos in range(3)]
    mass_diag = quadrature * (JACOBIAN / TIME_STEP)

    def squares_total(residual):
        return lax.psum(jnp.sum(node_share * residual * residual), ("ax", "circ", "gap"))

    rhs = wall_gate * assemble(quadrature * JACOBIAN * (w_old * (1.0 / TIME_STEP) + force))
    solution = jnp.zeros_like(rhs)
    residual = rhs
    direction = rhs
    norm_now = squares_total(residual)
    for iteration in range(ITERS):
        applied = mass_diag * direction
        for operate_axis_pos in range(3):
            inner_grad = local_derive(direction, diff_matrix, operate_axis_pos, False)
            applied = applied + local_derive(
                stiffness[operate_axis_pos] * inner_grad, diff_matrix, operate_axis_pos, True
            )
        image = wall_gate * assemble(applied)
        alpha = norm_now / lax.psum(jnp.sum(node_share * direction * image), ("ax", "circ", "gap"))
        solution = solution + alpha * direction
        residual = residual - alpha * image
        norm_next = squares_total(residual)
        direction = residual + norm_next / norm_now * direction
        norm_now = norm_next
    element_table = element_table_of(solution)
    fluid = sample_blocks(element_table, elements[0, 0, 0], state[0:3])
    kept = advance(state, fluid) * (1.0 - departed)[None, :]
    arrived = settle_arrivals(arrivals, element_table)
    return (solution, kept[None, None, None], arrived[None, None, None])


def solution(mesh):
    placed = (
        P("ax", "circ", "gap"),
        P("ax", "circ", "gap"),
        P("ax", "circ", "gap"),
        P("ax", "circ", "gap", None, None),
        P("ax", "circ", "gap", None, None),
        P("ax", "circ", "gap", None, None),
        P("ax", "circ", "gap", None),
        P("ax", "circ", "gap", None),
        P("ax", "circ", "gap", None, None),
        P("ax", "circ", "gap", None),
    )
    return jax.shard_map(
        shards,
        mesh=mesh,
        in_specs=placed,
        out_specs=(
            P("ax", "circ", "gap"),
            P("ax", "circ", "gap", None, None),
            P("ax", "circ", "gap", None, None, None),
        ),
        check_vma=False,
    )
```

profile of v0, /device:TPU:1, one launch (start us, length us, event | category | flops | bytes accessed | tf_op | source)
XLA Modules:
  0.0 936.1 jit_solution(17269371500699526761)
XLA Ops:
  2.6 4.0 collective-permute-start
  6.6 3.8 collective-permute-start.1
  16.7 2.9 collective-permute-start.2
  19.6 3.1 collective-permute-start.3
  23.8 2.2 collective-permute-start.4
  26.0 4.3 collective-permute-start.5
  48.1 4.6 collective-permute-start.7
  53.6 4.0 collective-permute-start.8
  57.6 2.7 collective-permute-start.9
  61.3 3.1 collective-permute-start.10
  64.4 3.9 collective-permute-start.11
  68.3 2.6 copy.239
  70.9 23.1 %gather_fusion.2 = f32[6144,9]{1,0:T(8,128)} fusion(f32[9,8192]{0,1:T(8,128)} %copy.239, s32[6144]{0:T(1024)S(1)} %broadcast_clamp_fusion), kind=kCustom, calls=%fused_computation.2 | custom fusion | bytes 466944 | tf_op jit(solution)/shard_map/jit(_take)/gather | solution.py:145
  94.0 2.4 copy.240
  107.3 104.3 %all-reduce.2 = (f32[]{:T(128)}, f32[]{:T(128)}) all-reduce(f32[]{:T(128)} %get-tuple-element.551, f32[]{:T(128)} %get-tuple-element.550), channel_id=1, replica_groups=mesh['ax'=8,'circ'=16,'gap'=4] {'ax','circ','gap'}, use_global_device_ids=true, to_apply=%region_5.6 | all-reduce | flops 2 | bytes 16 | tf_op jit(solution)/shard_map/psum | solution.py:295
  213.6 95.2 %psum.44 = f32[]{:T(128)} all-reduce(f32[]{:T(128)} %get-tuple-element.574), channel_id=1, replica_groups=mesh['ax'=8,'circ'=16,'gap'=4] {'ax','circ','gap'}, use_global_device_ids=true, to_apply=%region_13.14 | all-reduce | flops 1 | bytes 8 | tf_op jit(solution)/shard_map/psum | solution.py:295
  312.0 2.7 collective-permute-start.12
  314.7 3.8 collective-permute-start.13
  318.6 34.3 %gather_fusion.3 = s32[6144]{0:T(1024)S(1)} fusion(s32[8192]{0:T(1024)S(1)} %bitcast.357, s32[6144]{0:T(1024)S(1)} %broadcast_clamp_fusion), kind=kCustom, calls=%fused_computation.3 | custom fusion | bytes 73728 | tf_op jit(solution)/shard_map/jit(_take)/gather | solution.py:146
  355.1 2.6 collective-permute-done.15
  357.9 3.3 collective-permute-start.16
  361.2 3.4 collective-permute-start.17
  364.7 3.8 collective-permute-done.16
  381.1 97.3 %psum.45 = f32[]{:T(128)} all-reduce(f32[]{:T(128)} %fusion.29), channel_id=1, replica_groups=mesh['ax'=8,'circ'=16,'gap'=4] {'ax','circ','gap'}, use_global_device_ids=true, to_apply=%region_19.20 | all-reduce | flops 1 | bytes 8 | tf_op jit(solution)/shard_map/psum | solution.py:310
  480.5 95.0 %psum.46 = f32[]{:T(128)} all-reduce(f32[]{:T(128)} %fusion.26), channel_id=1, replica_groups=mesh['ax'=8,'circ'=16,'gap'=4] {'ax','circ','gap'}, use_global_device_ids=true, to_apply=%region_21.22 | all-reduce | flops 1 | bytes 8 | tf_op jit(solution)/shard_map/psum | solution.py:295
  578.7 4.2 collective-permute-start.18
  582.9 2.3 collective-permute-start.19
  585.3 3.0 collective-permute-start.24
  591.1 32.6 %scatter_custom_fusion.16 = f32[8192]{0:T(1024)S(1)} fusion(s32[6144]{0:T(1024)S(1)} %bitcast.386, f32[6144]{0:T(1024)S(1)} %reshape.5040, f32[]{:T(128)} %constant.831.clone.1), kind=kCustom, calls=%fused_computation.294 | custom fusion | flops 6144 | bytes 32772 | tf_op jit(solution)/shard_map/scatter-max | solution.py:151
  623.7 3.7 collective-permute-start.28
  636.6 4.3 collective-permute-start.22
  640.9 2.4 collective-permute-start.23
  645.1 3.4 collective-permute-done.23
  660.0 101.7 %psum.47 = f32[]{:T(128)} all-reduce(f32[]{:T(128)} %fusion.31), channel_id=1, replica_groups=mesh['ax'=8,'circ'=16,'gap'=4] {'ax','circ','gap'}, use_global_device_ids=true, to_apply=%region_27.28 | all-reduce | flops 1 | bytes 8 | tf_op jit(solution)/shard_map/psum | solution.py:310
  765.8 73.7 %while.51 = (s32[]{:T(128)}, f32[3,2048]{1,0:T(4,128)}, s32[3,2048]{1,0:T(4,128)}, f32[512,64]{0,1:T(8,128)S(1)}, f32[3,3,2048]{2,1,0:T(4,128)}, /*index=5*/s32[]{:T(128)}, s32[]{:T(128)}, s32[]{}, s32[]{}) while((s32[]{:T(128)}, f32[3,2048]{1,0:T(4,128)}, s32[3,2048]{1,0:T(4,128)}, f32[512,64]{0,1:T(8,128)S(1)}, f32[3,3,2048]{2,1,0:T(4,128)}, ...), condition=%wide.region_34.36_spmd, body=%wide.region_32.35_spmd.sunk | while | flops 4737028 | bytes 31297672 | solution.py:119
  767.5 2.5 broadcast_multiply_fusion.15
  770.0 5.3 copy.309
  776.2 8.9 gather_fusion.1
  785.1 3.9 fusion.122
  792.1 2.5 broadcast_multiply_fusion.15
  794.6 5.3 copy.309
  800.7 8.9 gather_fusion.1
  809.6 3.9 fusion.122
  816.7 2.5 broadcast_multiply_fusion.15
  819.2 5.3 copy.309
  825.3 8.9 gather_fusion.1
  834.2 3.9 fusion.122
  841.4 93.1 %while.50 = (s32[]{:T(128)}, f32[4,2048]{1,0:T(4,128)S(1)}, s32[4,2048]{1,0:T(4,128)}, f32[512,64]{0,1:T(8,128)S(1)}, f32[4,3,2048]{2,0,1:T(4,128)}, /*index=5*/s32[]{:T(128)}, s32[]{:T(128)}, s32[]{}, s32[]{}) while((s32[]{:T(128)}, f32[4,2048]{1,0:T(4,128)S(1)}, s32[4,2048]{1,0:T(4,128)}, f32[512,64]{0,1:T(8,128)S(1)}, ...), condition=%wide.region_30.32_spmd, body=%wide.region_28.31_spmd.sunk | while | flops 4737028 | bytes 31297672 | solution.py:119
  843.1 2.5 broadcast_multiply_fusion.13
  845.6 5.3 copy.308
  851.7 8.9 gather_fusion
  860.6 3.9 fusion.120
  866.4 2.5 broadcast_multiply_fusion.13
  868.8 5.3 copy.308
  875.0 8.9 gather_fusion
  883.9 3.9 fusion.120
  889.6 2.5 broadcast_multiply_fusion.13
  892.1 5.3 copy.308
  898.2 8.9 gather_fusion
  907.1 3.9 fusion.120
  912.9 2.5 broadcast_multiply_fusion.13
  915.3 5.3 copy.308
  921.5 8.9 gather_fusion
  930.4 3.9 fusion.120
  (379 shorter events, 111.5 us)
Async XLA Ops:
  0.6 317.9 %copy-start = (s32[1,1,1,8192]{3,2,1,0:T(1,128)S(1)}, s32[1,1,1,8192]{3,2,1,0:T(1,128)}, u32[]{:S(2)}) copy-start(s32[1,1,1,8192]{3,2,1,0:T(1,128)} %param.95) | copy-start | bytes 98308
  2.6 14.1 %collective-permute-start = (f32[1,32,128]{2,0,1:T(1,128)S(1)}, f32[1,32,128]{2,0,1:T(1,128)S(1)}, u32[]{:S(2)}, u32[]{:S(2)}) collective-permute-start(f32[1,32,128]{2,0,1:T(1,128)S(1)} %get-tuple-element.678), channel_id=1, source_target_pairs={{0,64},{64,128},{128,192},{192,256},{256,320},{320,384},{384,448},... | collective-permute-start | bytes 49160 | tf_op jit(solution)/shard_map/ppermute | solution.py:51
  6.6 10.0 %collective-permute-start.1 = (f32[1,32,128]{2,0,1:T(1,128)S(1)}, f32[1,32,128]{2,0,1:T(1,128)S(1)}, u32[]{:S(2)}, u32[]{:S(2)}) collective-permute-start(f32[1,32,128]{2,0,1:T(1,128)S(1)} %get-tuple-element.679), channel_id=1, source_target_pairs={{64,0},{128,64},{192,128},{256,192},{320,256},{384,320},{448,384},... | collective-permute-start | bytes 49160 | tf_op jit(solution)/shard_map/ppermute | solution.py:52
  16.7 6.7 collective-permute-start.2
  19.6 4.0 collective-permute-start.3
  22.8 356.2 %copy-start.20 = (s32[16]{0:T(128)}, s32[16]{0:T(128)S(1)}, u32[]{:S(2)}) copy-start(s32[16]{0:T(128)S(1)} %add_bitcast_fusion) | copy-start | bytes 196
  23.8 8.5 collective-permute-start.4
  26.0 7.8 collective-permute-start.5
  30.4 339.8 %copy-start.22 = (f32[10]{0:T(128)}, f32[10]{0:T(128)S(1)}, u32[]{:S(2)}) copy-start(f32[10]{0:T(128)S(1)} %get-tuple-element.683) | copy-start | bytes 124
  33.8 10.2 %copy-start.10 = (f32[32,32,1]{1,0,2:T(8,128)S(1)}, f32[32,32,1]{1,0,2:T(8,128)}, u32[]{:S(2)}) copy-start(f32[32,32,1]{1,0,2:T(8,128)} %constant.867) | copy-start | bytes 12292
  33.8 10.5 %copy-start.2 = (f32[8,32,128]{2,1,0:T(8,128)S(1)}, f32[8,32,128]{2,1,0:T(8,128)}, u32[]{:S(2)}) copy-start(f32[8,32,128]{2,1,0:T(8,128)} %param.88) | copy-start | bytes 393220
  33.8 10.5 %copy-start.3 = (f32[128,128,1]{1,0,2:T(8,128)S(1)}, f32[128,128,1]{1,0,2:T(8,128)}, u32[]{:S(2)}) copy-start(f32[128,128,1]{1,0,2:T(8,128)} %constant.868) | copy-start | bytes 196612
  33.8 10.6 %copy-start.14 = (f32[8,32,128]{2,1,0:T(8,128)S(1)}, f32[8,32,128]{2,1,0:T(8,128)}, u32[]{:S(2)}) copy-start(f32[8,32,128]{2,1,0:T(8,128)} %param.89) | copy-start | bytes 393220
  33.8 10.6 %copy-start.19 = (f32[128]{0:T(128)S(1)}, f32[128]{0:T(128)}, u32[]{:S(2)}) copy-start(f32[128]{0:T(128)} %constant.847.clone) | copy-start | bytes 1540
  34.3 10.8 %copy-start.15 = (f32[8,8,1]{1,0,2:T(8,128)S(1)}, f32[8,8,1]{1,0,2:T(8,128)}, u32[]{:S(2)}) copy-start(f32[8,8,1]{1,0,2:T(8,128)} %constant.866) | copy-start | bytes 772
  35.9 9.4 %copy-start.12 = (f32[32,32,1]{1,0,2:T(8,128)S(1)}, f32[32,32,1]{1,0,2:T(8,128)}, u32[]{:S(2)}) copy-start(f32[32,32,1]{1,0,2:T(8,128)} %constant.869) | copy-start | bytes 12292
  37.6 8.0 copy-start.16
  37.7 8.2 copy-start.7
  46.2 6.5 collective-permute-start.6
  48.1 5.4 collective-permute-start.7
  53.6 7.3 collective-permute-start.8
  57.6 3.5 collective-permute-start.9
  61.3 35.1 %collective-permute-start.10 = (f32[10,34,1]{2,0,1:T(8,128)S(1)}, f32[10,34,1]{2,0,1:T(8,128)S(1)}, u32[]{:S(2)}, u32[]{:S(2)}) collective-permute-start(f32[10,34,1]{2,0,1:T(8,128)S(1)} %get-tuple-element.642), channel_id=1, source_target_pairs={{0,1},{1,2},{2,3},{3,0},{4,5},{5,6},{6,7},{7,4},{8,9},{9,10},{10,1... | collective-permute-start | bytes 4088 | tf_op jit(solution)/shard_map/ppermute | solution.py:51
  64.4 32.0 %collective-permute-start.11 = (f32[10,34,1]{2,0,1:T(8,128)S(1)}, f32[10,34,1]{2,0,1:T(8,128)S(1)}, u32[]{:S(2)}, u32[]{:S(2)}) collective-permute-start(f32[10,34,1]{2,0,1:T(8,128)S(1)} %get-tuple-element.643), channel_id=1, source_target_pairs={{1,0},{2,1},{3,2},{0,3},{5,4},{6,5},{7,6},{4,7},{9,8},{10,9},{11,1... | collective-permute-start | bytes 4088 | tf_op jit(solution)/shard_map/ppermute | solution.py:52
  312.0 40.9 %collective-permute-start.12 = (f32[1,32,128]{2,0,1:T(1,128)S(1)}, f32[1,32,128]{2,0,1:T(1,128)S(1)}, u32[]{:S(2)}, u32[]{:S(2)}) collective-permute-start(f32[1,32,128]{2,0,1:T(1,128)S(1)} %get-tuple-element.674), channel_id=1, source_target_pairs={{0,64},{64,128},{128,192},{192,256},{256,320},{320,384},{384,448},... | collective-permute-start | bytes 49160 | tf_op jit(solution)/shard_map/ppermute | solution.py:51
  314.7 38.2 %collective-permute-start.13 = (f32[1,32,128]{2,0,1:T(1,128)S(1)}, f32[1,32,128]{2,0,1:T(1,128)S(1)}, u32[]{:S(2)}, u32[]{:S(2)}) collective-permute-start(f32[1,32,128]{2,0,1:T(1,128)S(1)} %get-tuple-element.675), channel_id=1, source_target_pairs={{64,0},{128,64},{192,128},{256,192},{320,256},{384,320},{448,384},... | collective-permute-start | bytes 49160 | tf_op jit(solution)/shard_map/ppermute | solution.py:52
  318.5 35.8 %copy-start.11 = (s32[1,1,1,6,1024]{4,2,3,1,0:T(1,128)S(1)}, s32[1,1,1,6,1024]{4,2,3,1,0:T(1,128)}, u32[]{:S(2)}) copy-start(s32[1,1,1,6,1024]{4,2,3,1,0:T(1,128)} %param.96) | copy-start | bytes 73732
  318.6 46.0 %copy-start.24 = (s32[1,1,1,6]{3,2,1,0:T(1,128)S(1)}, s32[1,1,1,6]{3,2,1,0:T(1,128)}, u32[]{:S(2)}) copy-start(s32[1,1,1,6]{3,2,1,0:T(1,128)} %param.97) | copy-start | bytes 76
  352.9 2.2 collective-permute-start.14
  354.4 3.4 collective-permute-start.15
  357.9 10.6 %collective-permute-start.16 = (f32[10,34,1]{2,0,1:T(8,128)S(1)}, f32[10,34,1]{2,0,1:T(8,128)S(1)}, u32[]{:S(2)}, u32[]{:S(2)}) collective-permute-start(f32[10,34,1]{2,0,1:T(8,128)S(1)} %get-tuple-element.638), channel_id=1, source_target_pairs={{0,1},{1,2},{2,3},{3,0},{4,5},{5,6},{6,7},{7,4},{8,9},{9,10},{10,1... | collective-permute-start | bytes 4088 | tf_op jit(solution)/shard_map/ppermute | solution.py:51
  361.2 8.9 collective-permute-start.17
  377.5 255.1 %copy-start.4 = (f32[1,1,1,3,8192]{4,2,3,1,0:T(1,128)S(1)}, f32[1,1,1,3,8192]{4,2,3,1,0:T(1,128)}, u32[]{:S(2)}) copy-start(f32[1,1,1,3,8192]{4,2,3,1,0:T(1,128)} %param.91) | copy-start | bytes 294916
  377.7 256.5 %copy-start.17 = (s32[1,1,1,8192]{3,2,1,0:T(1,128)S(1)}, s32[1,1,1,8192]{3,2,1,0:T(1,128)}, u32[]{:S(2)}) copy-start(s32[1,1,1,8192]{3,2,1,0:T(1,128)} %param.94) | copy-start | bytes 98308
  577.0 71.5 %copy-start.23 = (f32[10]{0:T(128)S(1)}, f32[10]{0:T(128)}, u32[]{:S(2)}) copy-start(f32[10]{0:T(128)} %copy-done.22) | copy-start | bytes 124
  578.7 44.9 %collective-permute-start.18 = (f32[1,32,128]{2,0,1:T(1,128)S(1)}, f32[1,32,128]{2,0,1:T(1,128)S(1)}, u32[]{:S(2)}, u32[]{:S(2)}) collective-permute-start(f32[1,32,128]{2,0,1:T(1,128)S(1)} %get-tuple-element.672), channel_id=1, source_target_pairs={{0,64},{64,128},{128,192},{192,256},{256,320},{320,384},{384,448},... | collective-permute-start | bytes 49160 | tf_op jit(solution)/shard_map/ppermute | solution.py:51
  582.9 40.8 %collective-permute-start.19 = (f32[1,32,128]{2,0,1:T(1,128)S(1)}, f32[1,32,128]{2,0,1:T(1,128)S(1)}, u32[]{:S(2)}, u32[]{:S(2)}) collective-permute-start(f32[1,32,128]{2,0,1:T(1,128)S(1)} %get-tuple-element.673), channel_id=1, source_target_pairs={{64,0},{128,64},{192,128},{256,192},{320,256},{384,320},{448,384},... | collective-permute-start | bytes 49160 | tf_op jit(solution)/shard_map/ppermute | solution.py:52
  585.3 42.1 %collective-permute-start.24 = (f32[11,1024]{1,0:T(8,128)S(1)}, f32[11,1024]{1,0:T(8,128)S(1)}, u32[]{:S(2)}, u32[]{:S(2)}) collective-permute-start(f32[11,1024]{1,0:T(8,128)S(1)} %get-tuple-element.629), channel_id=1, source_target_pairs={{0,64},{64,128},{128,192},{192,256},{256,320},{320,384},{384,448},... | collective-permute-start | bytes 135176 | tf_op jit(solution)/shard_map/ppermute | solution.py:60
  588.3 40.5 %collective-permute-start.25 = (f32[11,1024]{1,0:T(8,128)S(1)}, f32[11,1024]{1,0:T(8,128)S(1)}, u32[]{:S(2)}, u32[]{:S(2)}) collective-permute-start(f32[11,1024]{1,0:T(8,128)S(1)} %get-tuple-element.628), channel_id=1, source_target_pairs={{64,0},{128,64},{192,128},{256,192},{320,256},{384,320},{448,384},... | collective-permute-start | bytes 135176 | tf_op jit(solution)/shard_map/ppermute | solution.py:60
  589.6 41.1 %collective-permute-start.26 = (f32[11,1024]{1,0:T(8,128)S(1)}, f32[11,1024]{1,0:T(8,128)S(1)}, u32[]{:S(2)}, u32[]{:S(2)}) collective-permute-start(f32[11,1024]{1,0:T(8,128)S(1)} %get-tuple-element.627), channel_id=1, source_target_pairs={{0,4},{4,8},{8,12},{12,16},{16,20},{20,24},{24,28},{28,32},{32,36}... | collective-permute-start | bytes 135176 | tf_op jit(solution)/shard_map/ppermute | solution.py:65
  623.7 12.0 %collective-permute-start.27 = (f32[11,1024]{1,0:T(8,128)S(1)}, f32[11,1024]{1,0:T(8,128)S(1)}, u32[]{:S(2)}, u32[]{:S(2)}) collective-permute-start(f32[11,1024]{1,0:T(8,128)S(1)} %get-tuple-element.626), channel_id=1, source_target_pairs={{0,60},{4,0},{8,4},{12,8},{16,12},{20,16},{24,20},{28,24},{32,28},... | collective-permute-start | bytes 135176 | tf_op jit(solution)/shard_map/ppermute | solution.py:65
  623.7 12.0 %collective-permute-start.28 = (f32[11,1024]{1,0:T(8,128)S(1)}, f32[11,1024]{1,0:T(8,128)S(1)}, u32[]{:S(2)}, u32[]{:S(2)}) collective-permute-start(f32[11,1024]{1,0:T(8,128)S(1)} %get-tuple-element.625), channel_id=1, source_target_pairs={{0,1},{1,2},{2,3},{4,5},{5,6},{6,7},{8,9},{9,10},{10,11},{12,13},{... | collective-permute-start | bytes 135176 | tf_op jit(solution)/shard_map/ppermute | solution.py:60
  627.4 8.4 collective-permute-start.29
  628.8 7.6 collective-permute-start.20
  630.7 5.6 collective-permute-start.21
  636.4 20.9 %copy-start.21 = (s32[16]{0:T(128)S(1)}, s32[16]{0:T(128)}, u32[]{:S(2)}) copy-start(s32[16]{0:T(128)} %copy-done.20) | copy-start | bytes 196
  636.6 8.5 collective-permute-start.22
  640.9 7.6 collective-permute-start.23
  763.2 1.2 copy-start.8
  765.8 75.6 %copy-start.18 = (f32[4,2048]{1,0:T(4,128)S(1)}, f32[4,2048]{1,0:T(4,128)}, u32[]{:S(2)}) copy-start(f32[4,2048]{1,0:T(4,128)} %custom-call.10) | copy-start | bytes 98308
  841.4 93.2 %copy-start.5 = (f32[1,1,1,3,8192]{4,2,3,1,0:T(1,128)S(1)}, f32[1,1,1,3,8192]{4,2,3,1,0:T(1,128)}, u32[]{:S(2)}) copy-start(f32[1,1,1,3,8192]{4,2,3,1,0:T(1,128)} %param.91) | copy-start | bytes 294916
  841.4 93.2 %copy-start.6 = (f32[1,1,1,3,8192]{4,2,3,1,0:T(1,128)S(1)}, f32[1,1,1,3,8192]{4,2,3,1,0:T(1,128)}, u32[]{:S(2)}) copy-start(f32[1,1,1,3,8192]{4,2,3,1,0:T(1,128)} %param.92) | copy-start | bytes 294916
  841.4 93.5 %copy-start.9 = (f32[1,1,1,3,8192]{4,2,3,1,0:T(1,128)S(1)}, f32[1,1,1,3,8192]{4,2,3,1,0:T(1,128)}, u32[]{:S(2)}) copy-start(f32[1,1,1,3,8192]{4,2,3,1,0:T(1,128)} %param.93) | copy-start | bytes 294916
  841.4 93.6 %copy-start.13 = (f32[8192]{0:T(1024)S(1)}, f32[8192]{0:T(1024)}, u32[]{:S(2)}) copy-start(f32[8192]{0:T(1024)} %broadcast_subtract_fusion) | copy-start | bytes 98308
  934.5 1.4 copy-start.1
where the time goes:
time: 945 us; the launch traced here: 936 us
  blocking collectives  494 us (52%)
  local copies, waits for them, and re-layouts  209 us (22%)
  other arithmetic  115 us (12%)
  starting transfers between devices  82.4 us (9%)
  waiting for transfers between devices  19 us (2%)
  between operations  9.77 us (1%)
    psum x3, blocking collectives, squares_total(): lax.psum(jnp.sum(node_share * residual * residual), ('ax', 'circ', 'gap'))  295 us
    psum x2, blocking collectives, shards(): lax.psum(jnp.sum(node_share * direction * image), ('ax', 'circ', 'gap'))  199 us
    gather x7, local copies, waits for them, and re-layouts, sample_elements(): picked = jnp.take(element_table, element_ids, axis=1)  62.4 us
    mul x7, local copies, waits for them, and re-layouts, sample_elements(): basis_first[:, None, None, :] * basis_second[None, :, None, :]  37.4 us
    ppermute x12, starting transfers between devices, with_halo(): before = lax.ppermute(last, axis, up)  36.1 us
    ppermute x12, starting transfers between devices, with_halo(): after = lax.ppermute(first, axis, down)  35.5 us
    gather x1, local copies, waits for them, and re-layouts, pack_leaving(): jnp.take(new_ids, flat_slots).reshape(6, 1, capacity).astype(state.dtype)  34.3 us
    another operation x1, other arithmetic, pack_leaving(): jnp.zeros((state.shape[1],), state.dtype).at[flat_slots]  32.6 us
  transfers between devices with their start and end apart: 30, of which 13 were waited for; matrix products, arithmetic and copies ran while one was open for 11% of the time, Pallas kernels for 0%

commit v1 on v0

v1 whole, which is shorter than its diff:
```python
import functools
import jax, jax.numpy as jnp, numpy as np
from jax import lax
from jax.experimental import pallas as pl
from jax.experimental.pallas import tpu as pltpu
from jax.sharding import PartitionSpec as P

MESH = pl.DeviceIdType.MESH
GLL_NODES = np.array([-1.0,-0.8717401485096066,-0.5917001814331423,-0.2092992179024789,0.2092992179024789,0.5917001814331423,0.8717401485096066,1.0])

GLL_WEIGHTS = np.array([0.03571428571428571,0.2107042271435061,0.3411226924835044,0.4124587946587038,0.4124587946587038,0.3411226924835044,0.2107042271435061,0.03571428571428571])

def bary_weights():
    eye = np.eye(8, dtype=bool)
    diff = np.where(eye, 1.0, GLL_NODES[:, None] - GLL_NODES[None, :])
    return 1.0 / np.prod(diff, axis=1)

def pick(rows, lanes):
    return jnp.take_along_axis(rows, lanes, axis=1, mode="promise_in_bounds")

def pack_kernel(counts_ref, xi_ref, vel_ref, mom_ref, new_ref, slots_ref, buf_ref, dep_ref, st_ref, rows_ref):
    st_ref[0:3, :] = xi_ref[...]
    st_ref[3:6, :] = vel_ref[...]
    st_ref[6:9, :] = mom_ref[...]
    st_ref[9:10, :] = new_ref[...].astype(jnp.float32)
    for row in range(6):
        rows_ref[row] = slots_ref[row:row + 1, :]
    st_ref[10:16, :] = jnp.ones((6, 8192), jnp.float32)
    lane = lax.broadcasted_iota(jnp.int32, (8, 128), 1)

    @pl.loop(0, 48)
    def _(group):
        row = group // 8
        start = pl.multiple_of((group % 8) * 128, 128)
        slot = jnp.broadcast_to(rows_ref[row, :, pl.ds(start, 128)], (8, 128))
        block = lax.shift_right_logical(slot, 7)
        within = lax.bitwise_and(slot, 127)
        first = jnp.zeros((8, 128), jnp.float32)
        second = jnp.zeros((8, 128), jnp.float32)
        for h in range(64):
            here = block == h
            cols = slice(h * 128, (h + 1) * 128)
            first = jnp.where(here, pick(st_ref[0:8, cols], within), first)
            second = jnp.where(here, pick(st_ref[8:16, cols], within), second)
        live = (lane + start < counts_ref[row]).astype(jnp.float32)
        first = first * live
        second = second * live
        buf_ref[row, 0:8, pl.ds(start, 128)] = first
        buf_ref[row, 8:11, pl.ds(start, 128)] = second[0:3]

    sub64 = lax.broadcasted_iota(jnp.int32, (64, 1024), 0)
    sub128 = lax.broadcasted_iota(jnp.int32, (128, 1024), 0)
    lanes = lax.broadcasted_iota(jnp.int32, (1, 1024), 1)
    total = jnp.zeros((64, 128), jnp.float32)
    for row in range(6):
        slot = slots_ref[row:row + 1, :]
        block = jnp.where(lanes < counts_ref[row], lax.shift_right_logical(slot, 7), 64)
        within = lax.bitwise_and(slot, 127)
        blocks = jnp.where(sub64 == block, 1.0, 0.0).astype(jnp.bfloat16)
        places = jnp.where(sub128 == within, 1.0, 0.0).astype(jnp.bfloat16)
        total = total + lax.dot_general(blocks, places, (((1,), (1,)), ((), ())), preferred_element_type=jnp.float32)
    for row in range(64):
        dep_ref[row] = total[row:row + 1]

def pack(xi, vel, mom, new, slots, counts):
    return pl.pallas_call(
        pack_kernel,
        out_shape=(jax.ShapeDtypeStruct((6, 11, 1024), jnp.float32), jax.ShapeDtypeStruct((64, 1, 128), jnp.float32)),
        in_specs=[pl.BlockSpec(memory_space=pltpu.SMEM)] + [pl.BlockSpec(memory_space=pltpu.VMEM)] * 5,
        out_specs=(pl.BlockSpec(memory_space=pltpu.VMEM),) * 2,
        scratch_shapes=[pltpu.VMEM((16, 8192), jnp.float32), pltpu.VMEM((6, 1, 1024), jnp.int32)],
        name="pack",
    )(counts, xi, vel, mom, new, slots)

def ladder(x):
    d = [x - np.float32(n) for n in GLL_NODES]
    pre = [None] * 8
    suf = [None] * 8
    pre[1] = d[0]
    for k in range(2, 8):
        pre[k] = pre[k - 1] * d[k - 1]
    suf[6] = d[7]
    for k in range(5, -1, -1):
        suf[k] = suf[k + 1] * d[k + 1]
    return [suf[0]] + [pre[k] * suf[k] for k in range(1, 7)] + [pre[7]]

def settle_kernel(gate_ref, w_ref, perm_ref, bary_ref, other_ref, xi_ref, vel_ref, mom_ref, el_ref, dep_ref, arr_ref, w_out, kept_ref, arrived_ref, table_ref):
    w = w_ref[...]
    w_out[...] = w
    moved = jnp.dot(w, perm_ref[...], precision=lax.Precision.HIGHEST, preferred_element_type=jnp.float32)
    lane = lax.broadcasted_iota(jnp.int32, (8, 128), 1)
    region = lane // 16
    for i in range(8):
        for k in range(8):
            entry = jnp.zeros((8, 128), jnp.float32)
            for c in range(4):
                part = moved[i * 32 + c * 8:i * 32 + c * 8 + 8]
                shift = ((c - k) * 16) % 128
                if shift:
                    part = pltpu.roll(part, shift, 1)
                entry = jnp.where(region == c, part, entry)
            table_ref[i * 8 + k] = entry * bary_ref[i * 8 + k]

    def sample(ids, x1, x2, x3):
        ids = jnp.broadcast_to(ids, (8, 128))
        l1 = ladder(jnp.broadcast_to(x1, (8, 128)))
        l3 = ladder(jnp.broadcast_to(x3, (8, 128)))
        x2 = jnp.broadcast_to(x2, (8, 128))
        l2 = x2 - other_ref[0]
        for t in range(1, 7):
            l2 = l2 * (x2 - other_ref[t])
        total = None
        for i in range(8):
            line = None
            for k in range(8):
                term = pick(table_ref[i * 8 + k], ids) * l3[k]
                line = term if line is None else line + term
            line = line * l1[i]
            total = line if total is None else total + line
        return jnp.sum(total * l2, axis=0, keepdims=True)

    def update(xi, vel, fluid):
        axial = vel[0:1] + 0.4 * (fluid - vel[0:1])
        circ = vel[1:2] * (1.0 - 0.4)
        radial = vel[2:3] * (1.0 - 0.4)
        return [xi[0:1] + 0.25 * axial, xi[1:2] + 0.25 * circ, xi[2:3] + 1.0 * radial, axial, circ, radial]

    @pl.loop(0, 64)
    def _(group):
        cols = pl.ds(pl.multiple_of(group * 128, 128), 128)
        xi = xi_ref[:, cols]
        vel = vel_ref[:, cols]
        fluid = sample(el_ref[:, cols], xi[0:1], xi[1:2], xi[2:3])
        stay = 1.0 - dep_ref[group]
        for row, value in enumerate(update(xi, vel, fluid)):
            kept_ref[row:row + 1, cols] = value * stay
        kept_ref[6:9, cols] = mom_ref[:, cols] * stay

    @pl.loop(0, 48)
    def _(group):
        row = group // 8
        cols = pl.ds(pl.multiple_of((group % 8) * 128, 128), 128)
        state = arr_ref[row, 0:8, cols]
        rest = arr_ref[row, 8:11, cols]
        fluid = sample(rest[1:2].astype(jnp.int32), state[0:1], state[1:2], state[2:3])
        live = rest[2:3] * gate_ref[row]
        for at, value in enumerate(update(state[0:3], state[3:6], fluid)):
            arrived_ref[row, at:at + 1, cols] = value * live
        arrived_ref[row, 6:8, cols] = state[6:8] * live
        arrived_ref[row, 8:9, cols] = rest[0:1] * live

def settle_consts():
    perm = np.zeros((128, 128), np.float32)
    for g in range(16):
        for k in range(8):
            perm[g * 8 + k, k * 16 + g] = 1.0
    b = bary_weights()
    bary = np.broadcast_to((b[:, None, None] * b[None, :, None] * b[None, None, :]).reshape(64, 8, 1), (64, 8, 128)).astype(np.float32)
    other = np.stack([np.broadcast_to(np.roll(GLL_NODES, -t)[:, None], (8, 128)) for t in range(1, 8)]).astype(np.float32)
    return perm, bary, other

def settle(gate, w, xi, vel, mom, el, dep, arr):
    perm, bary, other = settle_consts()
    return pl.pallas_call(
        settle_kernel,
        out_shape=(jax.ShapeDtypeStruct((256, 128), jnp.float32), jax.ShapeDtypeStruct((9, 8192), jnp.float32), jax.ShapeDtypeStruct((6, 9, 1024), jnp.float32)),
        in_specs=[pl.BlockSpec(memory_space=pltpu.SMEM)] + [pl.BlockSpec(memory_space=pltpu.VMEM)] * 10,
        out_specs=(pl.BlockSpec(memory_space=pltpu.VMEM),) * 3,
        scratch_shapes=[pltpu.VMEM((64, 8, 128), jnp.float32)],
        name="settle",
    )(gate, w, perm, bary, other, xi, vel, mom, el, dep, arr)


def field_consts():
    b = bary_weights()
    eye = np.eye(8, dtype=bool)
    diff = np.where(eye, 1.0, GLL_NODES[:, None] - GLL_NODES[None, :])
    off = np.where(eye, 0.0, b[None, :] / b[:, None] / diff)
    d = (off - np.eye(8) * np.sum(off, axis=1)[:, None]).astype(np.float32)
    left = np.concatenate([np.kron(d, np.eye(32, dtype=np.float32)), np.kron(np.eye(32, dtype=np.float32), d)])
    right = 4.0 * np.kron(np.eye(16, dtype=np.float32), d.T)
    w8 = GLL_WEIGHTS.astype(np.float32)
    wr = (w8[:, None, None] * np.tile(w8, 4)[None, :, None]).reshape(256, 1)
    quad = wr * np.tile(w8, 16)[None, :]
    half = np.where((np.arange(8) == 0) | (np.arange(8) == 7), 0.5, 1.0)
    share = (half[:, None] * np.tile(half, 4)[None, :]).reshape(256, 1) * np.tile(half, 16)[None, :]
    r = np.arange(256)[:, None] % 32 + np.zeros((1, 128))
    c = np.arange(128)[None, :] + np.zeros((256, 1))
    masks = np.stack([(r % 8 == 0) & (r > 0), (r % 8 == 7) & (r < 31), (c % 8 == 0) & (c > 0), (c % 8 == 7) & (c < 127)])
    ends = np.zeros((8, 128))
    ends[0, 0] = 1.0
    ends[1, 127] = 1.0
    return [np.ascontiguousarray(t, dtype=np.float32) for t in (left, left.T, right, right.T, quad, share, masks, ends)]

def exact_dot(a, b, dims=((1,), (0,))):
    return lax.dot_general(a, b, (dims, ((), ())), precision=lax.Precision.HIGHEST, preferred_element_type=jnp.float32)

def flow_kernel(sizes, w_ref, yield_ref, force_ref, left_ref, left_t_ref, right_ref, right_t_ref, quad_ref, share_ref, masks_ref, ends_ref, buf_ref,
                out_ref, arr_ref, v_ref, f_ref, z_ref, edge_c, edge_e, edge_g, got_a, got_c, got_e, got_g, pair_ref, sum_ref, got_sum,
                send_sem, recv_sem, sum_send, sum_recv, mig_send, mig_recv):
    n_ax, n_circ, n_gap = sizes
    ax, circ, gap = lax.axis_index("ax"), lax.axis_index("circ"), lax.axis_index("gap")

    def at(da=0, dc=0, dg=0):
        place = {}
        if da:
            place["ax"] = lax.rem(ax + (da + n_ax), n_ax)
        if dc:
            place["circ"] = lax.rem(circ + (dc + n_circ), n_circ)
        if dg:
            place["gap"] = lax.rem(gap + (dg + n_gap), n_gap)
        return place

    peers = [at(da=o) for o in range(1, n_ax)] + [at(dc=o) for o in range(1, n_circ)] + [at(dg=o) for o in range(1, n_gap)]
    peers += [at(da=a, dc=c) for a in (-1, 1) for c in (-1, 1)]
    barrier = pltpu.get_barrier_semaphore()
    for peer in peers:
        pl.semaphore_signal(barrier, inc=1, device_id=peer, device_id_type=MESH)

    quad = quad_ref[...]
    row = lax.broadcasted_iota(jnp.int32, (256, 128), 0)
    col = lax.broadcasted_iota(jnp.int32, (256, 128), 1)
    at_wall = ((col == 0) & (gap == 0)) | ((col == 127) & (gap == n_gap - 1))
    wall = jnp.where(at_wall, 0.0, 1.0)
    share = share_ref[...] * jnp.where(at_wall, 2.0, 1.0)
    share = share * jnp.where(((row < 32) & (ax == 0)) | ((row >= 224) & (ax == n_ax - 1)), 2.0, 1.0)
    low_ax = jnp.where(ax == 0, 0.0, 1.0)
    high_ax = jnp.where(ax == n_ax - 1, 0.0, 1.0)
    low_gap = jnp.where(gap == 0, 0.0, 1.0)
    high_gap = jnp.where(gap == n_gap - 1, 0.0, 1.0)
    pair_ref[...] = jnp.zeros((8, 256), jnp.float32)

    def gather_inner(f):
        f = f + masks_ref[0] * pltpu.roll(f, 1, 0) + masks_ref[1] * pltpu.roll(f, 255, 0)
        return f + masks_ref[2] * pltpu.roll(f, 1, 1) + masks_ref[3] * pltpu.roll(f, 127, 1)

    def remote(src, dst, k, t, place):
        return pltpu.make_async_remote_copy(src_ref=src, dst_ref=dst, send_sem=send_sem.at[k, t], recv_sem=recv_sem.at[k, t],
                                            device_id=place, device_id_type=MESH)

    def first_phase(k, f):
        f = gather_inner(f)
        f_ref[k] = f
        z_ref[k] = f
        edge_c[k, 0] = f_ref[k, pl.ds(0, 8, stride=32), :]
        edge_c[k, 1] = f_ref[k, pl.ds(31, 8, stride=32), :]
        for e, at_row in enumerate((0, 31, 224, 255)):
            edge_e[k, e] = f_ref[k, at_row:at_row + 1, :]
        copies = [remote(f_ref.at[k, 0:32], got_a.at[k, 1], k, 0, at(da=-1)),
                  remote(f_ref.at[k, 224:256], got_a.at[k, 0], k, 1, at(da=1)),
                  remote(edge_c.at[k, 0], got_c.at[k, 1], k, 2, at(dc=-1)),
                  remote(edge_c.at[k, 1], got_c.at[k, 0], k, 3, at(dc=1))]
        for e in range(4):
            copies.append(remote(edge_e.at[k, e], got_e.at[k, 3 - e], k, 4 + e, at(da=1 if e >= 2 else -1, dc=1 if e % 2 else -1)))
        for copy in copies:
            copy.start()
        return copies

    def second_phase(k, copies):
        for copy in copies:
            copy.wait()
        z_ref[k, 0:32, :] = z_ref[k, 0:32, :] + got_a[k, 0] * low_ax
        z_ref[k, 224:256, :] = z_ref[k, 224:256, :] + got_a[k, 1] * high_ax
        z_ref[k, pl.ds(0, 8, stride=32), :] = z_ref[k, pl.ds(0, 8, stride=32), :] + got_c[k, 0]
        z_ref[k, pl.ds(31, 8, stride=32), :] = z_ref[k, pl.ds(31, 8, stride=32), :] + got_c[k, 1]
        for e, at_row in enumerate((0, 31, 224, 255)):
            z_ref[k, at_row:at_row + 1, :] = z_ref[k, at_row:at_row + 1, :] + got_e[k, e] * (low_ax if e < 2 else high_ax)
        z = z_ref[k]
        faces = exact_dot(ends_ref[...], z, ((1,), (1,)))
        edge_g[k, 0] = faces[0:1]
        edge_g[k, 1] = faces[1:2]
        copies = [remote(edge_g.at[k, 0], got_g.at[k, 1], k, 8, at(dg=-1)),
                  remote(edge_g.at[k, 1], got_g.at[k, 0], k, 9, at(dg=1))]
        for copy in copies:
            copy.start()
        for copy in copies:
            copy.wait()
        pair_ref[0:1, :] = got_g[k, 0] * low_gap
        pair_ref[1:2, :] = got_g[k, 1] * high_gap
        v_ref[k] = (z + exact_dot(pair_ref[...], ends_ref[...], ((0,), (0,)))) * wall

    rhs = quad * 0.25 * (4.0 * w_ref[...] + force_ref[...])
    pl.semaphore_wait(barrier, len(peers))
    moves = [at(da=1), at(da=-1), at(dc=1), at(dc=-1), at(dg=1), at(dg=-1)]
    moving = [pltpu.make_async_remote_copy(src_ref=buf_ref.at[r], dst_ref=arr_ref.at[r], send_sem=mig_send.at[r], recv_sem=mig_recv.at[r],
                                           device_id=place, device_id_type=MESH) for r, place in enumerate(moves)]
    copies = first_phase(0, rhs)
    for copy in moving:
        copy.start()

    w = w_ref[...]
    slopes = exact_dot(left_ref[...], w)
    slope_g = exact_dot(w, right_ref[...])
    squares = 1.0 + slopes[0:256] * slopes[0:256] + slopes[256:512] * slopes[256:512] + slope_g * slope_g
    stiff = quad * 0.25 * (0.05 + yield_ref[...] / jnp.sqrt(squares))
    second_phase(0, copies)

    def total(x):
        return jnp.sum(x, axis=0, keepdims=True)

    sums = []
    for k in range(3):
        v = v_ref[k]
        slopes = exact_dot(left_ref[...], v)
        slope_g = exact_dot(v, right_ref[...])
        first, second = slopes[0:256], slopes[256:512]
        sums.append(total(share * v * v))
        if k < 2:
            flux_g = stiff * slope_g
            flux = jnp.concatenate([stiff * first, stiff * second], axis=0)
            image = quad * v + exact_dot(left_t_ref[...], flux) + exact_dot(flux_g, right_t_ref[...])
            copies = first_phase(k + 1, image)
        sums.append(total(quad * v * v + stiff * (first * first + second * second + slope_g * slope_g)))
        if k < 2:
            second_phase(k + 1, copies)

    sub = lax.broadcasted_iota(jnp.int32, (8, 128), 0)
    part = lax.broadcasted_iota(jnp.int32, (8, 128), 1) // 16
    rows = jnp.zeros((8, 128), jnp.float32)
    for m, value in enumerate(sums):
        rows = jnp.where(sub == m, jnp.broadcast_to(value, (8, 128)), rows)
    for shift in (64, 32, 16):
        rows = rows + pltpu.roll(rows, shift, 1)
    line = jnp.sum(jnp.where(sub == part, rows, 0.0), axis=0, keepdims=True)
    slot = 0
    for stage, (name, count) in enumerate((("circ", n_circ), ("ax", n_ax), ("gap", n_gap))):
        sum_ref[stage] = line
        copies = []
        for o in range(1, count):
            place = {"circ": at(dc=o), "ax": at(da=o), "gap": at(dg=o)}[name]
            copies.append(pltpu.make_async_remote_copy(src_ref=sum_ref.at[stage], dst_ref=got_sum.at[slot], send_sem=sum_send.at[slot],
                                                       recv_sem=sum_recv.at[slot], device_id=place, device_id_type=MESH))
            slot += 1
        for copy in copies:
            copy.start()
        for copy in copies:
            copy.wait()
        for o in range(1, count):
            line = line + got_sum[slot - o]
    m = jnp.sum(jnp.where(sub == part, jnp.broadcast_to(line, (8, 128)), 0.0), axis=1, keepdims=True)
    m0, m1, m2, m3, m4, m5 = [m[i:i + 1, :] for i in range(6)]
    scale = m0 / m1
    m1 = m1 * scale
    m2 = m2 * scale * scale
    m3 = m3 * scale * scale * scale
    m4 = m4 * scale * scale * scale * scale
    m5 = m5 * scale * scale * scale * scale * scale

    def ratio(a, b):
        return jnp.where((a > 0.0) & (b > 0.0), a / b, 0.0)

    a0 = m0 / m1
    rr1 = a0 * a0 * m2 - m0
    e = 1.0 + rr1 / m0
    p1 = e * e * m1 - 2.0 * e * a0 * m2 + a0 * a0 * m3
    a1 = ratio(rr1, p1)
    c1 = a0 + a1 * e
    c2 = a0 * a1
    rr2 = m0 - 2.0 * c1 * m1 + (c1 * c1 + 2.0 * c2) * m2 - 2.0 * c1 * c2 * m3 + c2 * c2 * m4
    ra2 = m1 - 2.0 * c1 * m2 + (c1 * c1 + 2.0 * c2) * m3 - 2.0 * c1 * c2 * m4 + c2 * c2 * m5
    b1 = ratio(rr2, rr1)
    a2 = ratio(rr2, ra2 - b1 * ratio(rr2, a1))
    x0 = scale * (a0 + a1 * e + a2 * (1.0 + b1 * e))
    x1 = scale * scale * (-(c2 + a2 * (c1 + b1 * a0)))
    x2 = scale * scale * scale * (a2 * c2)
    out_ref[...] = x0 * v_ref[0] + x1 * v_ref[1] + x2 * v_ref[2]
    for copy in moving:
        copy.wait()

def flow(sizes, w, yld, force, buf):
    consts = field_consts()
    vm = lambda *s: pltpu.VMEM(s, jnp.float32)
    return pl.pallas_call(
        functools.partial(flow_kernel, sizes),
        out_shape=(jax.ShapeDtypeStruct((256, 128), jnp.float32), jax.ShapeDtypeStruct(buf.shape, jnp.float32)),
        in_specs=[pl.BlockSpec(memory_space=pltpu.VMEM)] * (3 + len(consts)) + [pl.BlockSpec(memory_space=pl.ANY)],
        out_specs=(pl.BlockSpec(memory_space=pltpu.VMEM), pl.BlockSpec(memory_space=pl.ANY)),
        scratch_shapes=[vm(3, 256, 128), vm(3, 256, 128), vm(3, 256, 128), vm(3, 2, 8, 128), vm(3, 4, 1, 128), vm(3, 2, 1, 256),
                        vm(3, 2, 32, 128), vm(3, 2, 8, 128), vm(3, 4, 1, 128), vm(3, 2, 1, 256), vm(8, 256), vm(3, 1, 128), vm(25, 1, 128),
                        pltpu.SemaphoreType.DMA((3, 10)), pltpu.SemaphoreType.DMA((3, 10)), pltpu.SemaphoreType.DMA((25,)),
                        pltpu.SemaphoreType.DMA((25,)), pltpu.SemaphoreType.DMA((6,)), pltpu.SemaphoreType.DMA((6,))],
        compiler_params=pltpu.CompilerParams(collective_id=0, has_side_effects=True),
        name="flow",
    )(w, yld, force, *consts, buf)


def solution(mesh):
    sizes = (mesh.shape["ax"], mesh.shape["circ"], mesh.shape["gap"])

    def shards(w_old, yield_stress, force, xi, vel, mom, el, new, slots, counts):
        flat = lambda t: t.reshape(256, 128)
        xi, vel, mom = [t.reshape(3, 8192) for t in (xi, vel, mom)]
        buf, dep = pack(xi, vel, mom, new.reshape(1, 8192), slots.reshape(6, 1024), counts.reshape(6))
        w, arr = flow(sizes, flat(w_old), flat(yield_stress), flat(force), buf)
        ax, gap = lax.axis_index("ax"), lax.axis_index("gap")
        ok = jnp.stack([ax > 0, ax < sizes[0] - 1, ax >= 0, ax >= 0, gap > 0, gap < sizes[2] - 1]).astype(jnp.float32)
        w_new, kept, arrived = settle(ok, w, xi, vel, mom, el.reshape(1, 8192), dep, arr)
        return w_new.reshape(w_old.shape), kept[None, None, None], arrived[None, None, None]

    spec = lambda n: P("ax", "circ", "gap", *([None] * n))
    return jax.shard_map(
        shards,
        mesh=mesh,
        in_specs=(spec(0), spec(0), spec(0), spec(2), spec(2), spec(2), spec(1), spec(1), spec(2), spec(1)),
        out_specs=(spec(0), spec(2), spec(3)),
        check_vma=False,
    )
```

time: 945 us -> 98.9 us (0.10)
  blocking collectives: 494 us -> 0 us
  local copies, waits for them, and re-layouts: 209 us -> 6.26 us
  other arithmetic: 115 us -> 0.58 us
  Pallas kernels: 0 us -> 90.4 us
  starting transfers between devices: 82.4 us -> 0 us
  waiting for transfers between devices: 19 us -> 0 us
    psum x5 -> x0, blocking collectives: 494 us -> none  [the longest x3 295 us: squares_total(): lax.psum(jnp.sum(node_share * residual * residual), ('ax', 'circ', 'gap'))]
    gather x10 -> x0, local copies, waits for them, and re-layouts: 122 us -> none  [the longest x7 62.4 us: sample_elements(): picked = jnp.take(element_table, element_ids, axis=1)]
    pallas_call x0 -> x3, Pallas kernels: none -> 90.4 us  [the longest x1 56.7 us: flow(): pl.pallas_call(functools.partial(flow_kernel, sizes), out_shape=(jax.Shap...]
    ppermute x30 -> x0, starting transfers between devices: 82.4 us -> none  [the longest x12 36.1 us: with_halo(): before = lax.ppermute(last, axis, up)]
    mul x7 -> x0, local copies, waits for them, and re-layouts: 37.4 us -> none  [sample_elements(): basis_first[:, None, None, :] * basis_second[None, :, None, :]]
    another operation x1 -> x0, other arithmetic: 32.6 us -> none  [pack_leaving(): jnp.zeros((state.shape[1],), state.dtype).at[flat_slots]]
    mul x36 -> x0, other arithmetic: 31.6 us -> none  [the longest x14 17.7 us: sample_elements(): basis_first[:, None, None, :] * basis_second[None, :, None, :]]
    reduce_sum x12 -> x0, other arithmetic: 31 us -> none  [the longest x7 27.4 us: sample_elements(): return jnp.sum(picked * combined, axis=0)]
  transfers between devices with their start and end apart: 30 -> 0, of which waited for: 13 -> 0; matrix products, arithmetic and copies ran while one was open for 11% -> 0% of each run, Pallas kernels for 0% -> 0%
where the time goes in v1:
time: 98.9 us; the launch traced here: 97.9 us
  Pallas kernels  90.4 us (91%)
  local copies, waits for them, and re-layouts  6.26 us (6%)
    pallas_call x1, Pallas kernels, flow(): pl.pallas_call(functools.partial(flow_kernel, sizes), out_shape=(jax.Shap...  56.7 us
    pallas_call x1, Pallas kernels, settle(): pl.pallas_call(settle_kernel, out_shape=(jax.ShapeDtypeStruct((256, 128),...  20.9 us
    pallas_call x1, Pallas kernels, pack(): pl.pallas_call(pack_kernel, out_shape=(jax.ShapeDtypeStruct((6, 11, 1024)...  12.8 us
    unnamed x13, local copies, waits for them, and re-layouts  6.16 us

profile of v1, /device:TPU:1, one launch (start us, length us, event | category | flops | bytes accessed | tf_op | source)
XLA Modules:
  0.0 97.9 jit_solution(3017696547943484672)
XLA Ops:
  0.6 0.0 copy-start.1
  0.7 0.1 stack.24
  0.8 0.6 convert_element_type.3.gate_ref
  1.3 1.4 %copy.35 = s32[1,1,1,6,1024]{4,3,2,1,0:T(8,128)} copy(s32[1,1,1,6,1024]{4,2,3,1,0:T(1,128)} %param.29) | data formatting | bytes 49152
  2.7 0.0 copy-done.1
  2.7 0.0 copy-start.2
  2.7 0.0 copy-start.3
  2.7 0.7 copy.34
  3.4 0.2 copy-done.2
  3.6 0.0 copy-done.3
  3.6 0.8 copy_bitcast_fusion
  4.5 12.8 %pack.1 = (f32[6,11,1024]{2,1,0:T(8,128)}, f32[64,1,128]{2,1,0:T(1,128)}) custom-call(s32[6]{0:T(128)} %bitcast.34, f32[3,8192]{1,0:T(4,128)} %bitcast.24, f32[3,8192]{1,0:T(4,128)} %get-tuple-element.21.vel_ref, f32[3,8192]{1,0:T(4,128)} %get-tuple-element.20.mom_ref, s32[1,8192]{1,0:T(1,128)} %bitcast.32, s32[6,1024]{1,0:T(8,128)} %bitcast.28), custom_call_target="tpu_custom_call" | custom-call | tf_op jit(solution)/shard_map/pack/pallas_call | solution.py:66
  17.2 56.7 %flow.1 = (f32[256,128]{1,0:T(8,128)}, f32[6,11,1024]{2,1,0:T(8,128)}) custom-call(f32[256,128]{1,0:T(8,128)} %bitcast.29, f32[256,128]{1,0:T(8,128)} %bitcast.30, f32[256,128]{1,0:T(8,128)} %bitcast.31, f32[512,256]{1,0:T(8,128)} %constant.38.clone.left_ref, f32[256,512]{1,0:T(8,128)} %constant.39.clone.left_t_ref, f32[128,128]{1,0:T(8,128)} %constant.40.clone.right_ref, ...), custom_call_target="tpu_custom_call" | custom-call | tf_op jit(solution)/shard_map/flow/pallas_call | solution.py:373
  74.0 20.9 %settle.1 = (f32[256,128]{1,0:T(8,128)}, f32[9,8192]{1,0:T(8,128)}, f32[6,9,1024]{2,1,0:T(8,128)}) custom-call(f32[6]{0:T(128)} %convert_element_type.3.gate_ref, f32[256,128]{1,0:T(8,128)} %get-tuple-element.11.w_ref, f32[128,128]{1,0:T(8,128)} %constant.46.clone.perm_ref, f32[64,8,128]{2,1,0:T(8,128)} %constant.47.clone.bary_ref, ...), custom_call_target="tpu_custom_call" | custom-call | tf_op jit(solution)/shard_map/settle/pallas_call | solution.py:164
  94.9 0.0 copy-start
  94.9 2.1 %copy.24 = f32[1,1,1,9,8192]{4,2,3,1,0:T(1,128)} copy(f32[1,1,1,9,8192]{4,3,2,1,0:T(8,128)} %bitcast.26) | data formatting | bytes 589824
  97.0 0.0 copy-done
  97.0 0.9 copy.25
Async XLA Ops:
  0.6 2.1 %copy-start.1 = (f32[1,1,1,3,8192]{4,2,3,1,0:T(1,128)S(1)}, f32[1,1,1,3,8192]{4,2,3,1,0:T(1,128)}, u32[]{:S(2)}) copy-start(f32[1,1,1,3,8192]{4,2,3,1,0:T(1,128)} %param.24) | copy-start | bytes 294916
  2.7 0.9 copy-start.2
  2.7 0.9 copy-start.3
  94.9 2.1 %copy-start = (f32[6,9,1024]{2,1,0:T(8,128)S(1)}, f32[6,9,1024]{2,1,0:T(8,128)}, u32[]{:S(2)}) copy-start(f32[6,9,1024]{2,1,0:T(8,128)} %get-tuple-element.16) | copy-start | bytes 663556

commit v2 on v1

v2 whole, which is shorter than its diff:
```python
import functools
import jax, jax.numpy as jnp, numpy as np
from jax import lax
from jax.experimental import pallas as pl
from jax.experimental.pallas import tpu as pltpu
from jax.sharding import PartitionSpec as P

MESH = pl.DeviceIdType.MESH
GLL_NODES = np.array([-1.0,-0.8717401485096066,-0.5917001814331423,-0.2092992179024789,0.2092992179024789,0.5917001814331423,0.8717401485096066,1.0])
GLL_WEIGHTS = np.array([0.03571428571428571,0.2107042271435061,0.3411226924835044,0.4124587946587038,0.4124587946587038,0.3411226924835044,0.2107042271435061,0.03571428571428571])

def bary_weights():
    eye = np.eye(8, dtype=bool)
    diff = np.where(eye, 1.0, GLL_NODES[:, None] - GLL_NODES[None, :])
    return 1.0 / np.prod(diff, axis=1)

def pick(rows, lanes):
    return jnp.take_along_axis(rows, lanes, axis=1, mode="promise_in_bounds")

def pick_row(rows, at):
    return jnp.take_along_axis(rows, at, axis=0, mode="promise_in_bounds")

def leaving_row(fields, slots_ref, count, row, buf_ref):
    lane = lax.broadcasted_iota(jnp.int32, (8, 128), 1)
    for s in range(8):
        slot = jnp.broadcast_to(slots_ref[row, s:s + 1, :], (8, 128))
        block = lax.shift_right_logical(slot, 10)
        inner = lax.bitwise_and(lax.shift_right_logical(slot, 7), 7)
        within = lax.bitwise_and(slot, 127)
        live = (lane + s * 128 < count).astype(jnp.float32)
        for f, field in enumerate(fields):
            found = None
            for b in range(8):
                got = pick(field(b), within)
                found = got if found is None else jnp.where(block == b, got, found)
            found = pick_row(found, inner) * live
            buf_ref[row, f, s:s + 1, :] = found[0:1]
        buf_ref[row, 10, s:s + 1, :] = live[0:1]

def departed_flags(slots_ref, counts_ref):
    sub64 = lax.broadcasted_iota(jnp.int32, (64, 128), 0)
    sub128 = lax.broadcasted_iota(jnp.int32, (128, 128), 0)
    lanes = lax.broadcasted_iota(jnp.int32, (1, 128), 1)

    def one(row, total):
        count = counts_ref[row]
        blocks, places = [], []
        for s in range(8):
            slot = slots_ref[row, s:s + 1, :]
            block = jnp.where(lanes + s * 128 < count, lax.shift_right_logical(slot, 7), 64)
            within = lax.bitwise_and(slot, 127)
            blocks.append(jnp.where(sub64 == block, 1.0, 0.0).astype(jnp.bfloat16))
            places.append(jnp.where(sub128 == within, 1.0, 0.0).astype(jnp.bfloat16))
        return total + lax.dot_general(jnp.concatenate(blocks, 1), jnp.concatenate(places, 1), (((1,), (1,)), ((), ())), preferred_element_type=jnp.float32)

    return lax.fori_loop(0, 6, one, jnp.zeros((64, 128), jnp.float32))

def pack_kernel(counts_ref, xi_ref, vel_ref, mom_ref, new_ref, slots_ref, buf_ref, dep_ref, id_ref):
    id_ref[...] = new_ref[...].astype(jnp.float32)
    fields = [lambda b, ref=ref, d=d: ref[d, b * 8:b * 8 + 8, :] for ref in (xi_ref, vel_ref, mom_ref) for d in range(3)]
    fields.append(lambda b: id_ref[b * 8:b * 8 + 8, :])

    @pl.loop(0, 6)
    def _(row):
        leaving_row(fields, slots_ref, counts_ref[row], row, buf_ref)

    dep_ref[...] = departed_flags(slots_ref, counts_ref)

def pack(xi, vel, mom, new, slots, counts):
    return pl.pallas_call(
        pack_kernel,
        out_shape=(jax.ShapeDtypeStruct((6, 11, 8, 128), jnp.float32), jax.ShapeDtypeStruct((64, 128), jnp.float32)),
        in_specs=[pl.BlockSpec(memory_space=pltpu.SMEM)] + [pl.BlockSpec(memory_space=pltpu.VMEM)] * 5,
        out_specs=(pl.BlockSpec(memory_space=pltpu.VMEM),) * 2,
        scratch_shapes=[pltpu.VMEM((64, 128), jnp.float32)],
        name="pack",
    )(counts, xi, vel, mom, new, slots)

def ladder(x):
    d = [x - np.float32(n) for n in GLL_NODES]
    pre = [None] * 8
    suf = [None] * 8
    pre[1] = d[0]
    for k in range(2, 8):
        pre[k] = pre[k - 1] * d[k - 1]
    suf[6] = d[7]
    for k in range(5, -1, -1):
        suf[k] = suf[k + 1] * d[k + 1]
    return [suf[0]] + [pre[k] * suf[k] for k in range(1, 7)] + [pre[7]]

def settle_kernel(gate_ref, w_ref, bary_ref, xi_ref, vel_ref, mom_ref, el_ref, dep_ref, arr_ref, w_out, kept_ref, arrived_ref, table_ref, basis_ref, fluid_ref):
    w = w_ref[...]
    w_out[...] = w
    w = w * bary_ref[...]
    high = w.astype(jnp.bfloat16)
    low = (w - high.astype(jnp.float32)).astype(jnp.bfloat16)
    table_ref[:, 0:128] = high
    table_ref[:, 128:256] = low
    table_ref[:, 256:384] = high
    lane_g = lax.broadcasted_iota(jnp.int32, (128, 128), 0) // 8

    def sample(ids, x1, x2, x3):
        for k, value in enumerate(ladder(x1)):
            basis_ref[0, k * 8:k * 8 + 8, :] = value
        for k, value in enumerate(ladder(x2)):
            basis_ref[1, k * 8:k * 8 + 8, :] = value
        for k, value in enumerate(ladder(x3)):
            rounded = value.astype(jnp.bfloat16).astype(jnp.float32)
            basis_ref[2, k * 8:k * 8 + 8, :] = rounded
            basis_ref[3, k * 8:k * 8 + 8, :] = value - rounded
        circ = lax.shift_right_logical(ids, 4)
        radial = lax.bitwise_and(ids, 15)
        for q in range(4):
            right, weights = [], []
            for s in (2 * q, 2 * q + 1):
                mine = lane_g == jnp.broadcast_to(radial[s:s + 1], (128, 128))
                b_high = jnp.where(mine, jnp.concatenate([basis_ref[2, pl.ds(s, 8, stride=8), :]] * 16, axis=0), 0.0).astype(jnp.bfloat16)
                b_low = jnp.where(mine, jnp.concatenate([basis_ref[3, pl.ds(s, 8, stride=8), :]] * 16, axis=0), 0.0).astype(jnp.bfloat16)
                right.append(jnp.concatenate([b_high, b_high, b_low], axis=0))
                second = basis_ref[1, pl.ds(s, 8, stride=8), :]
                cc = jnp.broadcast_to(circ[s:s + 1], (8, 128))
                weights.append([jnp.where(cc == c, second, 0.0) for c in range(4)])
            values = jnp.dot(table_ref[...], jnp.concatenate(right, axis=1), preferred_element_type=jnp.float32)
            for h, s in enumerate((2 * q, 2 * q + 1)):
                total = None
                for i in range(8):
                    line = None
                    for c in range(4):
                        term = values[i * 32 + c * 8:i * 32 + c * 8 + 8, h * 128:h * 128 + 128] * weights[h][c]
                        line = term if line is None else line + term
                    line = line * jnp.broadcast_to(basis_ref[0, i * 8 + s:i * 8 + s + 1, :], (8, 128))
                    total = line if total is None else total + line
                fluid_ref[s:s + 1, :] = jnp.sum(total, axis=0, keepdims=True)
        return fluid_ref[...]

    def update(xi, vel, fluid):
        axial = vel[0] + 0.4 * (fluid - vel[0])
        circ = vel[1] * (1.0 - 0.4)
        radial = vel[2] * (1.0 - 0.4)
        return [xi[0] + 0.25 * axial, xi[1] + 0.25 * circ, xi[2] + 1.0 * radial, axial, circ, radial]

    @pl.loop(0, 8)
    def _(block):
        rows = pl.ds(pl.multiple_of(block * 8, 8), 8)
        xi = [xi_ref[d, rows, :] for d in range(3)]
        fluid = sample(el_ref[rows, :], *xi)
        stay = 1.0 - dep_ref[rows, :]
        for at, value in enumerate(update(xi, [vel_ref[d, rows, :] for d in range(3)], fluid)):
            kept_ref[at, rows, :] = value * stay
        for d in range(3):
            kept_ref[6 + d, rows, :] = mom_ref[d, rows, :] * stay

    @pl.loop(0, 6)
    def _(row):
        state = [arr_ref[row, d] for d in range(11)]
        fluid = sample(state[9].astype(jnp.int32), *state[0:3])
        live = state[10] * gate_ref[row]
        for at, value in enumerate(update(state[0:3], state[3:6], fluid) + state[6:9]):
            arrived_ref[row, at] = value * live

def settle(gate, w, xi, vel, mom, el, dep, arr):
    b = bary_weights()
    rows = (b[:, None, None] * np.ones((1, 4, 1)) * b[None, None, :]).reshape(256, 1)
    bary = np.ascontiguousarray(rows * np.tile(b, 16)[None, :], dtype=np.float32)
    return pl.pallas_call(
        settle_kernel,
        out_shape=(jax.ShapeDtypeStruct((256, 128), jnp.float32), jax.ShapeDtypeStruct((9, 64, 128), jnp.float32), jax.ShapeDtypeStruct((6, 9, 8, 128), jnp.float32)),
        in_specs=[pl.BlockSpec(memory_space=pltpu.SMEM)] + [pl.BlockSpec(memory_space=pltpu.VMEM)] * 8,
        out_specs=(pl.BlockSpec(memory_space=pltpu.VMEM),) * 3,
        scratch_shapes=[pltpu.VMEM((256, 384), jnp.bfloat16), pltpu.VMEM((4, 64, 128), jnp.float32), pltpu.VMEM((8, 128), jnp.float32)],
        name="settle",
    )(gate, w, bary, xi, vel, mom, el, dep, arr)

def diff_table():
    b = bary_weights()
    eye = np.eye(8, dtype=bool)
    diff = np.where(eye, 1.0, GLL_NODES[:, None] - GLL_NODES[None, :])
    off = np.where(eye, 0.0, b[None, :] / b[:, None] / diff)
    return (off - np.eye(8) * np.sum(off, axis=1)[:, None]).astype(np.float32)

def pieces(a, count=2):
    parts = []
    rest = a.astype(np.float32)
    for _ in range(count):
        part = rest.astype(jnp.bfloat16)
        parts.append(part)
        rest = rest - part.astype(np.float32)
    return parts

def field_consts():
    d = diff_table()
    eye = np.eye(16, dtype=np.float32)

    def left(m):
        h, l = pieces(np.kron(eye, m))
        return np.block([[h, h], [l, l]])

    def right(m):
        h, l = pieces(4.0 * np.kron(eye, m))
        return np.block([[h, l], [h, l]])

    w8 = GLL_WEIGHTS.astype(np.float32)
    half = np.where((np.arange(8) == 0) | (np.arange(8) == 7), 0.5, 1.0)
    r = np.arange(32)[:, None] + np.zeros((1, 128))
    c = np.arange(128)[None, :] + np.zeros((32, 1))
    small = np.stack([np.tile(w8, 4)[:, None] * np.tile(w8, 16)[None, :], np.tile(half, 4)[:, None] * np.tile(half, 16)[None, :],
                      (r % 8 == 0) & (r > 0), (r % 8 == 7) & (r < 31), (c % 8 == 0) & (c > 0), (c % 8 == 7) & (c < 127)]).astype(np.float32)
    ends = np.zeros((8, 384), np.float32)
    for piece in range(3):
        ends[0, piece * 128] = 1.0
        ends[1, piece * 128 + 127] = 1.0
    spread = np.zeros((32, 128), np.float32)
    for piece in range(3):
        spread[piece * 8, 0] = 1.0
        spread[piece * 8 + 1, 127] = 1.0
    bf = lambda t: np.ascontiguousarray(t).astype(jnp.bfloat16)
    return [bf(left(d)), bf(left(d.T)), bf(right(d.T)), bf(right(d)), small, bf(ends), bf(spread)]

def halves(x):
    high = x.astype(jnp.bfloat16)
    return high, (x - high.astype(jnp.float32)).astype(jnp.bfloat16)

def thirds(x):
    high, rest = x.astype(jnp.bfloat16), None
    rest = x - high.astype(jnp.float32)
    mid = rest.astype(jnp.bfloat16)
    return high, mid, (rest - mid.astype(jnp.float32)).astype(jnp.bfloat16)

def mix(a, b, dims=((1,), (0,))):
    return lax.dot_general(a, b, (dims, ((), ())), preferred_element_type=jnp.float32)

def along_circ(x, left):
    x = jnp.concatenate([x[0:128], x[128:256]], axis=1)
    y = mix(left, jnp.concatenate(halves(x), axis=0))
    y = y[0:128] + y[128:256]
    return jnp.concatenate([y[:, 0:128], y[:, 128:256]], axis=0)

def along_gap(x, right):
    y = mix(jnp.concatenate(halves(x), axis=1), right)
    return y[:, 0:128] + y[:, 128:256]

def along_ax(x, d):
    x = [x[i * 32:i * 32 + 32] for i in range(8)]
    even = [x[j] + x[7 - j] for j in range(4)]
    odd = [x[j] - x[7 - j] for j in range(4)]
    out = [None] * 8
    for i in range(4):
        a = b = None
        for j in range(4):
            p = np.float32(0.5 * (float(d[i, j]) - float(d[i, 7 - j]))) * odd[j]
            q = np.float32(0.5 * (float(d[i, j]) + float(d[i, 7 - j]))) * even[j]
            a = p if a is None else a + p
            b = q if b is None else b + q
        out[i] = a + b
        out[7 - i] = a - b
    return jnp.concatenate(out, axis=0)

def flow_kernel(sizes, w_ref, yield_ref, force_ref, lc_ref, lct_ref, rg_ref, rgt_ref, small_ref, ends_ref, spread_ref, buf_ref,
                out_ref, arr_ref, v_ref, f_ref, z_ref, quad_ref, stiff_ref, edge_c, edge_e, edge_g, got_a, got_c, got_e, got_g, pair_ref, sum_ref, got_sum,
                send_sem, recv_sem, sum_send, sum_recv, mig_send, mig_recv):
    n_ax, n_circ, n_gap = sizes
    d8 = diff_table()
    ax, circ, gap = lax.axis_index("ax"), lax.axis_index("circ"), lax.axis_index("gap")

    def at(da=0, dc=0, dg=0):
        place = {}
        if da:
            place["ax"] = lax.rem(ax + (da + n_ax), n_ax)
        if dc:
            place["circ"] = lax.rem(circ + (dc + n_circ), n_circ)
        if dg:
            place["gap"] = lax.rem(gap + (dg + n_gap), n_gap)
        return place

    peers = [at(da=o) for o in range(1, n_ax)] + [at(dc=o) for o in range(1, n_circ)] + [at(dg=o) for o in range(1, n_gap)]
    peers += [at(da=a, dc=c) for a in (-1, 1) for c in (-1, 1)]
    barrier = pltpu.get_barrier_semaphore()
    for peer in peers:
        pl.semaphore_signal(barrier, inc=1, device_id=peer, device_id_type=MESH)

    weights = GLL_WEIGHTS.astype(np.float32)
    quad = jnp.concatenate([small_ref[0] * weights[i] for i in range(8)], axis=0)
    quad_ref[...] = quad
    col = lax.broadcasted_iota(jnp.int32, (32, 128), 1)
    at_wall = ((col == 0) & (gap == 0)) | ((col == 127) & (gap == n_gap - 1))
    wall = jnp.where(at_wall, 0.0, 1.0)
    share = small_ref[1] * jnp.where(at_wall, 2.0, 1.0)
    low_ax = jnp.where(ax == 0, 0.0, 1.0)
    high_ax = jnp.where(ax == n_ax - 1, 0.0, 1.0)
    low_gap = jnp.where(gap == 0, 0.0, 1.0)
    high_gap = jnp.where(gap == n_gap - 1, 0.0, 1.0)
    ax_share = [jnp.where(ax == 0, 1.0, 0.5)] + [1.0] * 6 + [jnp.where(ax == n_ax - 1, 1.0, 0.5)]
    pair_ref[...] = jnp.zeros((8, 256), jnp.float32)

    def every(tile):
        return jnp.concatenate([tile] * 8, axis=0)

    def gather_inner(f):
        f = f + every(small_ref[2]) * pltpu.roll(f, 1, 0) + every(small_ref[3]) * pltpu.roll(f, 255, 0)
        return f + every(small_ref[4]) * pltpu.roll(f, 1, 1) + every(small_ref[5]) * pltpu.roll(f, 127, 1)

    def remote(src, dst, k, t, place):
        return pltpu.make_async_remote_copy(src_ref=src, dst_ref=dst, send_sem=send_sem.at[k, t], recv_sem=recv_sem.at[k, t],
                                            device_id=place, device_id_type=MESH)

    def stage(k, f):
        f = gather_inner(f)
        f_ref[k] = f
        z_ref[k] = f
        edge_c[k, 0] = f_ref[k, pl.ds(0, 8, stride=32), :]
        edge_c[k, 1] = f_ref[k, pl.ds(31, 8, stride=32), :]
        for e, at_row in enumerate((0, 31, 224, 255)):
            edge_e[k, e] = f_ref[k, at_row:at_row + 1, :]

    def first_phase(k):
        copies = [remote(edge_e.at[k, e], got_e.at[k, 3 - e], k, 4 + e, at(da=1 if e >= 2 else -1, dc=1 if e % 2 else -1)) for e in range(4)]
        copies += [remote(edge_c.at[k, 0], got_c.at[k, 1], k, 2, at(dc=-1)),
                   remote(edge_c.at[k, 1], got_c.at[k, 0], k, 3, at(dc=1)),
                   remote(f_ref.at[k, 0:32], got_a.at[k, 1], k, 0, at(da=-1)),
                   remote(f_ref.at[k, 224:256], got_a.at[k, 0], k, 1, at(da=1))]
        for copy in copies:
            copy.start()
        return copies

    def second_phase(k, copies):
        for copy in copies:
            copy.wait()
        z_ref[k, 0:32, :] = z_ref[k, 0:32, :] + got_a[k, 0] * low_ax
        z_ref[k, 224:256, :] = z_ref[k, 224:256, :] + got_a[k, 1] * high_ax
        z_ref[k, pl.ds(0, 8, stride=32), :] = z_ref[k, pl.ds(0, 8, stride=32), :] + got_c[k, 0]
        z_ref[k, pl.ds(31, 8, stride=32), :] = z_ref[k, pl.ds(31, 8, stride=32), :] + got_c[k, 1]
        for e, at_row in enumerate((0, 31, 224, 255)):
            z_ref[k, at_row:at_row + 1, :] = z_ref[k, at_row:at_row + 1, :] + got_e[k, e] * (low_ax if e < 2 else high_ax)
        z = z_ref[k]
        faces = mix(ends_ref[...], jnp.concatenate(thirds(z), axis=1), ((1,), (1,)))
        edge_g[k, 0] = faces[0:1]
        edge_g[k, 1] = faces[1:2]
        copies = [remote(edge_g.at[k, 0], got_g.at[k, 1], k, 8, at(dg=-1)),
                  remote(edge_g.at[k, 1], got_g.at[k, 0], k, 9, at(dg=1))]
        for copy in copies:
            copy.start()
        for copy in copies:
            copy.wait()
        pair_ref[0:1, :] = got_g[k, 0] * low_gap
        pair_ref[1:2, :] = got_g[k, 1] * high_gap
        pair = pair_ref[...]
        pair = jnp.concatenate(thirds(pair) + (jnp.zeros((8, 256), jnp.bfloat16),), axis=0)
        v_ref[k] = (z_ref[k] + mix(pair, spread_ref[...], ((0,), (0,)))) * every(wall)

    stage(0, quad * 0.25 * (4.0 * w_ref[...] + force_ref[...]))
    pl.semaphore_wait(barrier, len(peers))
    moves = [at(da=1), at(da=-1), at(dc=1), at(dc=-1), at(dg=1), at(dg=-1)]
    moving = [pltpu.make_async_remote_copy(src_ref=buf_ref.at[r], dst_ref=arr_ref.at[r], send_sem=mig_send.at[r], recv_sem=mig_recv.at[r],
                                           device_id=place, device_id_type=MESH) for r, place in enumerate(moves)]
    copies = first_phase(0)
    for copy in moving:
        copy.start()

    w = w_ref[...]
    slope_a, slope_c, slope_g = along_ax(w, d8), along_circ(w, lc_ref[...]), along_gap(w, rg_ref[...])
    squares = 1.0 + slope_a * slope_a + slope_c * slope_c + slope_g * slope_g
    stiff_ref[...] = quad * 0.25 * (0.05 + yield_ref[...] / jnp.sqrt(squares))
    second_phase(0, copies)

    def total(x):
        return jnp.sum(x.reshape(32, 8, 128), axis=0)

    sums = []
    for k in range(3):
        v = v_ref[k]
        stiff = stiff_ref[...]
        slope_a, slope_c, slope_g = along_ax(v, d8), along_circ(v, lc_ref[...]), along_gap(v, rg_ref[...])
        if k < 2:
            image = quad_ref[...] * v + along_ax(stiff * slope_a, d8.T)
            image = image + along_circ(stiff * slope_c, lct_ref[...]) + along_gap(stiff * slope_g, rgt_ref[...])
            stage(k + 1, image)
            copies = first_phase(k + 1)
        square = v * v
        sums.append(total(jnp.concatenate([square[i * 32:i * 32 + 32] * (share * ax_share[i]) for i in range(8)], axis=0)))
        sums.append(total(quad_ref[...] * square + stiff * (slope_a * slope_a + slope_c * slope_c + slope_g * slope_g)))
        if k < 2:
            second_phase(k + 1, copies)

    sub = lax.broadcasted_iota(jnp.int32, (8, 128), 0)
    part = lax.broadcasted_iota(jnp.int32, (8, 128), 1) // 16
    rows = jnp.zeros((8, 128), jnp.float32)
    for m, value in enumerate(sums):
        rows = jnp.where(sub == m, jnp.broadcast_to(jnp.sum(value, axis=0, keepdims=True), (8, 128)), rows)
    for shift in (64, 32, 16):
        rows = rows + pltpu.roll(rows, shift, 1)
    line = jnp.sum(jnp.where(sub == part, rows, 0.0), axis=0, keepdims=True)
    slot = 0
    for step, (name, count) in enumerate((("circ", n_circ), ("ax", n_ax), ("gap", n_gap))):
        sum_ref[step] = line
        copies = []
        for o in range(1, count):
            place = {"circ": at(dc=o), "ax": at(da=o), "gap": at(dg=o)}[name]
            copies.append(pltpu.make_async_remote_copy(src_ref=sum_ref.at[step], dst_ref=got_sum.at[slot], send_sem=sum_send.at[slot],
                                                       recv_sem=sum_recv.at[slot], device_id=place, device_id_type=MESH))
            slot += 1
        for copy in copies:
            copy.start()
        for copy in copies:
            copy.wait_recv()
        for o in range(1, count):
            line = line + got_sum[slot - o]
        for copy in copies:
            copy.wait_send()
    m = jnp.sum(jnp.where(sub == part, jnp.broadcast_to(line, (8, 128)), 0.0), axis=1, keepdims=True)
    m0, m1, m2, m3, m4, m5 = [m[i:i + 1, :] for i in range(6)]
    scale = m0 / m1
    m1 = m1 * scale
    m2 = m2 * scale * scale
    m3 = m3 * scale * scale * scale
    m4 = m4 * scale * scale * scale * scale
    m5 = m5 * scale * scale * scale * scale * scale

    def ratio(a, b):
        return jnp.where((a > 0.0) & (b > 0.0), a / b, 0.0)

    a0 = m0 / m1
    rr1 = a0 * a0 * m2 - m0
    e = 1.0 + rr1 / m0
    p1 = e * e * m1 - 2.0 * e * a0 * m2 + a0 * a0 * m3
    a1 = ratio(rr1, p1)
    c1 = a0 + a1 * e
    c2 = a0 * a1
    rr2 = m0 - 2.0 * c1 * m1 + (c1 * c1 + 2.0 * c2) * m2 - 2.0 * c1 * c2 * m3 + c2 * c2 * m4
    ra2 = m1 - 2.0 * c1 * m2 + (c1 * c1 + 2.0 * c2) * m3 - 2.0 * c1 * c2 * m4 + c2 * c2 * m5
    b1 = ratio(rr2, rr1)
    a2 = ratio(rr2, ra2 - b1 * ratio(rr2, a1))
    x0 = scale * (a0 + a1 * e + a2 * (1.0 + b1 * e))
    x1 = scale * scale * (-(c2 + a2 * (c1 + b1 * a0)))
    x2 = scale * scale * scale * (a2 * c2)
    out_ref[...] = x0 * v_ref[0] + x1 * v_ref[1] + x2 * v_ref[2]
    for copy in moving:
        copy.wait()

def flow(sizes, w, yld, force, buf):
    consts = field_consts()
    vm = lambda *s: pltpu.VMEM(s, jnp.float32)
    sums = sum(sizes) - 3
    return pl.pallas_call(
        functools.partial(flow_kernel, sizes),
        out_shape=(jax.ShapeDtypeStruct((256, 128), jnp.float32), jax.ShapeDtypeStruct(buf.shape, jnp.float32)),
        in_specs=[pl.BlockSpec(memory_space=pltpu.VMEM)] * (3 + len(consts)) + [pl.BlockSpec(memory_space=pl.ANY)],
        out_specs=(pl.BlockSpec(memory_space=pltpu.VMEM), pl.BlockSpec(memory_space=pl.ANY)),
        scratch_shapes=[vm(3, 256, 128), vm(3, 256, 128), vm(3, 256, 128), vm(256, 128), vm(256, 128), vm(3, 2, 8, 128), vm(3, 4, 1, 128), vm(3, 2, 1, 256),
                        vm(3, 2, 32, 128), vm(3, 2, 8, 128), vm(3, 4, 1, 128), vm(3, 2, 1, 256), vm(8, 256), vm(3, 1, 128), vm(sums, 1, 128),
                        pltpu.SemaphoreType.DMA((3, 10)), pltpu.SemaphoreType.DMA((3, 10)), pltpu.SemaphoreType.DMA((sums,)),
                        pltpu.SemaphoreType.DMA((sums,)), pltpu.SemaphoreType.DMA((6,)), pltpu.SemaphoreType.DMA((6,))],
        compiler_params=pltpu.CompilerParams(collective_id=0, has_side_effects=True),
        name="flow",
    )(w, yld, force, *consts, buf)

def solution(mesh):
    sizes = (mesh.shape["ax"], mesh.shape["circ"], mesh.shape["gap"])

    def shards(w_old, yield_stress, force, xi, vel, mom, el, new, slots, counts):
        flat = lambda t: t.reshape(256, 128)
        xi, vel, mom = [t.reshape(3, 64, 128) for t in (xi, vel, mom)]
        buf, dep = pack(xi, vel, mom, new.reshape(64, 128), slots.reshape(6, 8, 128), counts.reshape(6))
        w, arr = flow(sizes, flat(w_old), flat(yield_stress), flat(force), buf)
        ax, gap = lax.axis_index("ax"), lax.axis_index("gap")
        ok = jnp.stack([ax > 0, ax < sizes[0] - 1, ax >= 0, ax >= 0, gap > 0, gap < sizes[2] - 1]).astype(jnp.float32)
        w_new, kept, arrived = settle(ok, w, xi, vel, mom, el.reshape(64, 128), dep, arr)
        return w_new.reshape(w_old.shape), kept.reshape(1, 1, 1, 9, 8192), arrived.reshape(1, 1, 1, 6, 9, 1024)

    spec = lambda n: P("ax", "circ", "gap", *([None] * n))
    return jax.shard_map(
        shards,
        mesh=mesh,
        in_specs=(spec(0), spec(0), spec(0), spec(2), spec(2), spec(2), spec(1), spec(1), spec(2), spec(1)),
        out_specs=(spec(0), spec(2), spec(3)),
        check_vma=False,
    )
```

time: 98.9 us -> 70.1 us (0.71)
  Pallas kernels: 90.4 us -> 67.9 us
  local copies, waits for them, and re-layouts: 6.26 us -> 0.1 us
    pallas_call x1, Pallas kernels: 20.9 us -> 8.73 us  [settle(): pl.pallas_call(settle_kernel, out_shape=(jax.ShapeDtypeStruct((256, 128),...]
    unnamed x13 -> x0, local copies, waits for them, and re-layouts: 6.16 us -> none
    pallas_call x1, Pallas kernels: 12.8 us -> 7.54 us  [pack(): pl.pallas_call(pack_kernel, out_shape=(jax.ShapeDtypeStruct((6, 11, 8, 12...]
    pallas_call x1, Pallas kernels: 56.7 us -> 51.6 us  [flow(): pl.pallas_call(functools.partial(flow_kernel, sizes), out_shape=(jax.Shap...]
where the time goes in v2:
time: 70.1 us; the launch traced here: 69.2 us
  Pallas kernels  67.9 us (97%)
    pallas_call x1, Pallas kernels, flow(): pl.pallas_call(functools.partial(flow_kernel, sizes), out_shape=(jax.Shap...  51.6 us
    pallas_call x1, Pallas kernels, settle(): pl.pallas_call(settle_kernel, out_shape=(jax.ShapeDtypeStruct((256, 128),...  8.73 us
    pallas_call x1, Pallas kernels, pack(): pl.pallas_call(pack_kernel, out_shape=(jax.ShapeDtypeStruct((6, 11, 8, 12...  7.54 us

profile of v2, /device:TPU:1, one launch (start us, length us, event | category | flops | bytes accessed | tf_op | source)
XLA Modules:
  0.0 69.2 jit_solution(4648570921391504909)
XLA Ops:
  0.6 0.1 stack.24
  0.7 0.5 convert_element_type.3.gate_ref
  1.3 7.5 %pack.1 = (f32[6,11,8,128]{3,2,1,0:T(8,128)}, f32[64,128]{1,0:T(8,128)}) custom-call(s32[6]{0:T(128)} %bitcast.30, f32[3,64,128]{2,1,0:T(8,128)} %bitcast.18, f32[3,64,128]{2,1,0:T(8,128)} %bitcast.20, f32[3,64,128]{2,1,0:T(8,128)} %bitcast.22, s32[64,128]{1,0:T(8,128)} %bitcast.28, s32[6,8,128]{2,1,0:T(8,128)} %bitcast.29), custom_call_target="tpu_custom_call" | custom-call | tf_op jit(solution)/shard_map/pack/pallas_call | solution.py:70
  8.8 51.6 %flow.1 = (f32[256,128]{1,0:T(8,128)}, f32[6,11,8,128]{3,2,1,0:T(8,128)}) custom-call(f32[256,128]{1,0:T(8,128)} %bitcast.24, f32[256,128]{1,0:T(8,128)} %bitcast.25, f32[256,128]{1,0:T(8,128)} %bitcast.26, bf16[256,256]{1,0:T(8,128)(2,1)} %constant.32.clone.lc_ref, bf16[256,256]{1,0:T(8,128)(2,1)} %constant.33.clone.lct_ref, ...), custom_call_target="tpu_custom_call" | custom-call | tf_op jit(solution)/shard_map/flow/pallas_call | solution.py:443
  60.4 8.7 %settle.1 = (f32[256,128]{1,0:T(8,128)}, f32[9,64,128]{2,1,0:T(8,128)}, f32[6,9,8,128]{3,2,1,0:T(8,128)}) custom-call(f32[6]{0:T(128)} %convert_element_type.3.gate_ref, f32[256,128]{1,0:T(8,128)} %get-tuple-element.11.w_ref, f32[256,128]{1,0:T(8,128)} %constant.39.clone.bary_ref, f32[3,64,128]{2,1,0:T(8,128)} %bitcast.19, f32[3,64,128]{2,1,0:T(8,128)} %bitcast.21, ...), custom_call_target="tpu_custom_call" | custom-call | tf_op jit(solution)/shard_map/settle/pallas_call | solution.py:165

commit v3 on v2

--- a/solution.py
+++ b/solution.py
@@ -55,27 +55,6 @@
 
     return lax.fori_loop(0, 6, one, jnp.zeros((64, 128), jnp.float32))
 
-def pack_kernel(counts_ref, xi_ref, vel_ref, mom_ref, new_ref, slots_ref, buf_ref, dep_ref, id_ref):
-    id_ref[...] = new_ref[...].astype(jnp.float32)
-    fields = [lambda b, ref=ref, d=d: ref[d, b * 8:b * 8 + 8, :] for ref in (xi_ref, vel_ref, mom_ref) for d in range(3)]
-    fields.append(lambda b: id_ref[b * 8:b * 8 + 8, :])
-
-    @pl.loop(0, 6)
-    def _(row):
-        leaving_row(fields, slots_ref, counts_ref[row], row, buf_ref)
-
-    dep_ref[...] = departed_flags(slots_ref, counts_ref)
-
-def pack(xi, vel, mom, new, slots, counts):
-    return pl.pallas_call(
-        pack_kernel,
-        out_shape=(jax.ShapeDtypeStruct((6, 11, 8, 128), jnp.float32), jax.ShapeDtypeStruct((64, 128), jnp.float32)),
-        in_specs=[pl.BlockSpec(memory_space=pltpu.SMEM)] + [pl.BlockSpec(memory_space=pltpu.VMEM)] * 5,
-        out_specs=(pl.BlockSpec(memory_space=pltpu.VMEM),) * 2,
-        scratch_shapes=[pltpu.VMEM((64, 128), jnp.float32)],
-        name="pack",
-    )(counts, xi, vel, mom, new, slots)
-
 def ladder(x):
     d = [x - np.float32(n) for n in GLL_NODES]
     pre = [None] * 8
@@ -88,7 +67,7 @@
         suf[k] = suf[k + 1] * d[k + 1]
     return [suf[0]] + [pre[k] * suf[k] for k in range(1, 7)] + [pre[7]]
 
-def settle_kernel(gate_ref, w_ref, bary_ref, xi_ref, vel_ref, mom_ref, el_ref, dep_ref, arr_ref, w_out, kept_ref, arrived_ref, table_ref, basis_ref, fluid_ref):
+def settle_kernel(sizes, w_ref, bary_ref, xi_ref, vel_ref, mom_ref, el_ref, dep_ref, arr_ref, w_out, kept_ref, arrived_ref, table_ref, basis_ref, fluid_ref):
     w = w_ref[...]
     w_out[...] = w
     w = w * bary_ref[...]
@@ -150,26 +129,29 @@
         for d in range(3):
             kept_ref[6 + d, rows, :] = mom_ref[d, rows, :] * stay
 
+    ax, gap = lax.axis_index("ax"), lax.axis_index("gap")
+
     @pl.loop(0, 6)
     def _(row):
+        absent = ((row == 0) & (ax == 0)) | ((row == 1) & (ax == sizes[0] - 1)) | ((row == 4) & (gap == 0)) | ((row == 5) & (gap == sizes[2] - 1))
         state = [arr_ref[row, d] for d in range(11)]
         fluid = sample(state[9].astype(jnp.int32), *state[0:3])
-        live = state[10] * gate_ref[row]
+        live = state[10] * jnp.where(absent, 0.0, 1.0)
         for at, value in enumerate(update(state[0:3], state[3:6], fluid) + state[6:9]):
             arrived_ref[row, at] = value * live
 
-def settle(gate, w, xi, vel, mom, el, dep, arr):
+def settle(sizes, w, xi, vel, mom, el, dep, arr):
     b = bary_weights()
     rows = (b[:, None, None] * np.ones((1, 4, 1)) * b[None, None, :]).reshape(256, 1)
     bary = np.ascontiguousarray(rows * np.tile(b, 16)[None, :], dtype=np.float32)
     return pl.pallas_call(
-        settle_kernel,
+        functools.partial(settle_kernel, sizes),
         out_shape=(jax.ShapeDtypeStruct((256, 128), jnp.float32), jax.ShapeDtypeStruct((9, 64, 128), jnp.float32), jax.ShapeDtypeStruct((6, 9, 8, 128), jnp.float32)),
-        in_specs=[pl.BlockSpec(memory_space=pltpu.SMEM)] + [pl.BlockSpec(memory_space=pltpu.VMEM)] * 8,
+        in_specs=[pl.BlockSpec(memory_space=pltpu.VMEM)] * 8,
         out_specs=(pl.BlockSpec(memory_space=pltpu.VMEM),) * 3,
         scratch_shapes=[pltpu.VMEM((256, 384), jnp.bfloat16), pltpu.VMEM((4, 64, 128), jnp.float32), pltpu.VMEM((8, 128), jnp.float32)],
         name="settle",
-    )(gate, w, bary, xi, vel, mom, el, dep, arr)
+    )(w, bary, xi, vel, mom, el, dep, arr)
 
 def diff_table():
     b = bary_weights()
@@ -255,8 +237,8 @@
         out[7 - i] = a - b
     return jnp.concatenate(out, axis=0)
 
-def flow_kernel(sizes, w_ref, yield_ref, force_ref, lc_ref, lct_ref, rg_ref, rgt_ref, small_ref, ends_ref, spread_ref, buf_ref,
-                out_ref, arr_ref, v_ref, f_ref, z_ref, quad_ref, stiff_ref, edge_c, edge_e, edge_g, got_a, got_c, got_e, got_g, pair_ref, sum_ref, got_sum,
+def flow_kernel(sizes, w_ref, yield_ref, force_ref, lc_ref, lct_ref, rg_ref, rgt_ref, small_ref, ends_ref, spread_ref, counts_ref, xi_ref, vel_ref, mom_ref, new_ref, slots_ref,
+                out_ref, arr_ref, dep_ref, v_ref, f_ref, z_ref, quad_ref, stiff_ref, edge_c, edge_e, edge_g, got_a, got_c, got_e, got_g, pair_ref, sum_ref, got_sum, buf_ref, id_ref,
                 send_sem, recv_sem, sum_send, sum_recv, mig_send, mig_recv):
     n_ax, n_circ, n_gap = sizes
     d8 = diff_table()
@@ -272,8 +254,8 @@
             place["gap"] = lax.rem(gap + (dg + n_gap), n_gap)
         return place
 
-    peers = [at(da=o) for o in range(1, n_ax)] + [at(dc=o) for o in range(1, n_circ)] + [at(dg=o) for o in range(1, n_gap)]
-    peers += [at(da=a, dc=c) for a in (-1, 1) for c in (-1, 1)]
+    around = [(a, c, g) for a in (0, -1, 1) for c in (0, -1, 1) for g in (0, -1, 1) if (a, c, g) != (0, 0, 0)]
+    peers = [at(*d) for d in around] + [at(da=o) for o in range(2, n_ax - 1)] + [at(dc=o) for o in range(2, n_circ - 1)] + [at(dg=o) for o in range(2, n_gap - 1)]
     barrier = pltpu.get_barrier_semaphore()
     for peer in peers:
         pl.semaphore_signal(barrier, inc=1, device_id=peer, device_id_type=MESH)
@@ -312,7 +294,7 @@
         for e, at_row in enumerate((0, 31, 224, 255)):
             edge_e[k, e] = f_ref[k, at_row:at_row + 1, :]
 
-    def first_phase(k):
+    def send(k):
         copies = [remote(edge_e.at[k, e], got_e.at[k, 3 - e], k, 4 + e, at(da=1 if e >= 2 else -1, dc=1 if e % 2 else -1)) for e in range(4)]
         copies += [remote(edge_c.at[k, 0], got_c.at[k, 1], k, 2, at(dc=-1)),
                    remote(edge_c.at[k, 1], got_c.at[k, 0], k, 3, at(dc=1)),
@@ -320,47 +302,79 @@
                    remote(f_ref.at[k, 224:256], got_a.at[k, 0], k, 1, at(da=1))]
         for copy in copies:
             copy.start()
-        return copies
-
-    def second_phase(k, copies):
+        faces = mix(ends_ref[...], jnp.concatenate(thirds(f_ref[k]), axis=1), ((1,), (1,)))
+        for s in range(2):
+            for h in range(2):
+                edge_g[k, s, h] = faces[s:s + 1, h * 128:h * 128 + 128]
+        later = []
+        for s in range(2):
+            dg = 1 if s else -1
+            t = 8 + 9 * s
+            for a in (-1, 1):
+                for c in (-1, 1):
+                    slot = 8 + (2 if a < 0 else 0) + (1 if c < 0 else 0)
+                    later.append(remote(edge_g.at[k, s, 1 if a > 0 else 0], got_g.at[k, 1 - s, slot], k, t + slot - 3, at(da=a, dc=c, dg=dg)))
+            for a in (-1, 1):
+                slot = 7 if a < 0 else 6
+                later.append(remote(edge_g.at[k, s, 1 if a > 0 else 0], got_g.at[k, 1 - s, slot], k, t + slot - 3, at(da=a, dg=dg)))
+            for c in (0, -1, 1):
+                slot = {0: 0, 1: 1, -1: 2}[c]
+                later.append(remote(edge_g.at[k, s], got_g.at[k, 1 - s, 2 * slot:2 * slot + 2], k, t + slot, at(dc=c, dg=dg)))
+        for copy in later:
+            copy.start()
+        return copies + later
+
+    lane = lax.broadcasted_iota(jnp.int32, (1, 128), 1)
+    place_of = lax.bitwise_and(lane, 31)
+
+    def receive(k, copies):
         for copy in copies:
-            copy.wait()
+            copy.wait_recv()
         z_ref[k, 0:32, :] = z_ref[k, 0:32, :] + got_a[k, 0] * low_ax
         z_ref[k, 224:256, :] = z_ref[k, 224:256, :] + got_a[k, 1] * high_ax
         z_ref[k, pl.ds(0, 8, stride=32), :] = z_ref[k, pl.ds(0, 8, stride=32), :] + got_c[k, 0]
         z_ref[k, pl.ds(31, 8, stride=32), :] = z_ref[k, pl.ds(31, 8, stride=32), :] + got_c[k, 1]
         for e, at_row in enumerate((0, 31, 224, 255)):
             z_ref[k, at_row:at_row + 1, :] = z_ref[k, at_row:at_row + 1, :] + got_e[k, e] * (low_ax if e < 2 else high_ax)
-        z = z_ref[k]
-        faces = mix(ends_ref[...], jnp.concatenate(thirds(z), axis=1), ((1,), (1,)))
-        edge_g[k, 0] = faces[0:1]
-        edge_g[k, 1] = faces[1:2]
-        copies = [remote(edge_g.at[k, 0], got_g.at[k, 1], k, 8, at(dg=-1)),
-                  remote(edge_g.at[k, 1], got_g.at[k, 0], k, 9, at(dg=1))]
-        for copy in copies:
-            copy.start()
-        for copy in copies:
-            copy.wait()
-        pair_ref[0:1, :] = got_g[k, 0] * low_gap
-        pair_ref[1:2, :] = got_g[k, 1] * high_gap
+        for s in range(2):
+            def moved(slot, shift, keep):
+                return jnp.where(keep, pltpu.roll(got_g[k, s, slot], shift, 1), 0.0)
+
+            low = moved(6, 32, lane < 32) + moved(8, 1, lane == 0) + moved(9, 63, lane == 31)
+            high = moved(7, 96, lane >= 96) + moved(10, 65, lane == 96) + moved(11, 127, lane == 127)
+            sides = []
+            for h, extra in ((0, low * low_ax), (1, high * high_ax)):
+                sides.append(got_g[k, s, h] + moved(2 + h, 97, place_of == 0) + moved(4 + h, 31, place_of == 31) + extra)
+            for h in range(2):
+                pair_ref[s:s + 1, h * 128:h * 128 + 128] = sides[h] * (high_gap if s else low_gap)
         pair = pair_ref[...]
         pair = jnp.concatenate(thirds(pair) + (jnp.zeros((8, 256), jnp.bfloat16),), axis=0)
         v_ref[k] = (z_ref[k] + mix(pair, spread_ref[...], ((0,), (0,)))) * every(wall)
 
-    stage(0, quad * 0.25 * (4.0 * w_ref[...] + force_ref[...]))
-    pl.semaphore_wait(barrier, len(peers))
+    id_ref[...] = new_ref[...].astype(jnp.float32)
+    fields = [lambda b, ref=ref, d=d: ref[d, b * 8:b * 8 + 8, :] for ref in (xi_ref, vel_ref, mom_ref) for d in range(3)]
+    fields.append(lambda b: id_ref[b * 8:b * 8 + 8, :])
     moves = [at(da=1), at(da=-1), at(dc=1), at(dc=-1), at(dg=1), at(dg=-1)]
     moving = [pltpu.make_async_remote_copy(src_ref=buf_ref.at[r], dst_ref=arr_ref.at[r], send_sem=mig_send.at[r], recv_sem=mig_recv.at[r],
                                            device_id=place, device_id_type=MESH) for r, place in enumerate(moves)]
-    copies = first_phase(0)
-    for copy in moving:
-        copy.start()
-
+
+    def pack_rows(first, last):
+        @pl.loop(first, last)
+        def _(row):
+            leaving_row(fields, slots_ref, counts_ref[row], row, buf_ref)
+
+        for copy in moving[first:last]:
+            copy.start()
+
+    stage(0, quad * 0.25 * (4.0 * w_ref[...] + force_ref[...]))
+    pl.semaphore_wait(barrier, len(peers))
+    copies = send(0)
     w = w_ref[...]
     slope_a, slope_c, slope_g = along_ax(w, d8), along_circ(w, lc_ref[...]), along_gap(w, rg_ref[...])
     squares = 1.0 + slope_a * slope_a + slope_c * slope_c + slope_g * slope_g
     stiff_ref[...] = quad * 0.25 * (0.05 + yield_ref[...] / jnp.sqrt(squares))
-    second_phase(0, copies)
+    pack_rows(0, 3)
+    receive(0, copies)
 
     def total(x):
         return jnp.sum(x.reshape(32, 8, 128), axis=0)
@@ -374,12 +388,18 @@
             image = quad_ref[...] * v + along_ax(stiff * slope_a, d8.T)
             image = image + along_circ(stiff * slope_c, lct_ref[...]) + along_gap(stiff * slope_g, rgt_ref[...])
             stage(k + 1, image)
-            copies = first_phase(k + 1)
+            sent, copies = copies, send(k + 1)
         square = v * v
         sums.append(total(jnp.concatenate([square[i * 32:i * 32 + 32] * (share * ax_share[i]) for i in range(8)], axis=0)))
         sums.append(total(quad_ref[...] * square + stiff * (slope_a * slope_a + slope_c * slope_c + slope_g * slope_g)))
+        if k == 0:
+            pack_rows(3, 6)
+        if k == 1:
+            dep_ref[...] = departed_flags(slots_ref, counts_ref)
         if k < 2:
-            second_phase(k + 1, copies)
+            for copy in sent:
+                copy.wait_send()
+            receive(k + 1, copies)
 
     sub = lax.broadcasted_iota(jnp.int32, (8, 128), 0)
     part = lax.broadcasted_iota(jnp.int32, (8, 128), 1) // 16
@@ -392,19 +412,22 @@
     slot = 0
     for step, (name, count) in enumerate((("circ", n_circ), ("ax", n_ax), ("gap", n_gap))):
         sum_ref[step] = line
-        copies = []
+        rounds = []
         for o in range(1, count):
             place = {"circ": at(dc=o), "ax": at(da=o), "gap": at(dg=o)}[name]
-            copies.append(pltpu.make_async_remote_copy(src_ref=sum_ref.at[step], dst_ref=got_sum.at[slot], send_sem=sum_send.at[slot],
+            rounds.append(pltpu.make_async_remote_copy(src_ref=sum_ref.at[step], dst_ref=got_sum.at[slot], send_sem=sum_send.at[slot],
                                                        recv_sem=sum_recv.at[slot], device_id=place, device_id_type=MESH))
             slot += 1
-        for copy in copies:
+        for copy in rounds:
             copy.start()
-        for copy in copies:
+        if step == 0:
+            for copy in copies:
+                copy.wait_send()
+        for copy in rounds:
             copy.wait_recv()
         for o in range(1, count):
             line = line + got_sum[slot - o]
-        for copy in copies:
+        for copy in rounds:
             copy.wait_send()
     m = jnp.sum(jnp.where(sub == part, jnp.broadcast_to(line, (8, 128)), 0.0), axis=1, keepdims=True)
     m0, m1, m2, m3, m4, m5 = [m[i:i + 1, :] for i in range(6)]
@@ -436,22 +459,24 @@
     for copy in moving:
         copy.wait()
 
-def flow(sizes, w, yld, force, buf):
+def flow(sizes, w, yld, force, xi, vel, mom, new, slots, counts):
     consts = field_consts()
     vm = lambda *s: pltpu.VMEM(s, jnp.float32)
     sums = sum(sizes) - 3
+    whole = pl.BlockSpec(memory_space=pltpu.VMEM)
     return pl.pallas_call(
         functools.partial(flow_kernel, sizes),
-        out_shape=(jax.ShapeDtypeStruct((256, 128), jnp.float32), jax.ShapeDtypeStruct(buf.shape, jnp.float32)),
-        in_specs=[pl.BlockSpec(memory_space=pltpu.VMEM)] * (3 + len(consts)) + [pl.BlockSpec(memory_space=pl.ANY)],
-        out_specs=(pl.BlockSpec(memory_space=pltpu.VMEM), pl.BlockSpec(memory_space=pl.ANY)),
-        scratch_shapes=[vm(3, 256, 128), vm(3, 256, 128), vm(3, 256, 128), vm(256, 128), vm(256, 128), vm(3, 2, 8, 128), vm(3, 4, 1, 128), vm(3, 2, 1, 256),
-                        vm(3, 2, 32, 128), vm(3, 2, 8, 128), vm(3, 4, 1, 128), vm(3, 2, 1, 256), vm(8, 256), vm(3, 1, 128), vm(sums, 1, 128),
-                        pltpu.SemaphoreType.DMA((3, 10)), pltpu.SemaphoreType.DMA((3, 10)), pltpu.SemaphoreType.DMA((sums,)),
+        out_shape=(jax.ShapeDtypeStruct((256, 128), jnp.float32), jax.ShapeDtypeStruct((6, 11, 8, 128), jnp.float32), jax.ShapeDtypeStruct((64, 128), jnp.float32)),
+        in_specs=[whole] * (3 + len(consts)) + [pl.BlockSpec(memory_space=pltpu.SMEM)] + [whole] * 5,
+        out_specs=(whole, pl.BlockSpec(memory_space=pl.ANY), whole),
+        scratch_shapes=[vm(3, 256, 128), vm(3, 256, 128), vm(3, 256, 128), vm(256, 128), vm(256, 128), vm(3, 2, 8, 128), vm(3, 4, 1, 128), vm(3, 2, 2, 1, 128),
+                        vm(3, 2, 32, 128), vm(3, 2, 8, 128), vm(3, 4, 1, 128), vm(3, 2, 12, 1, 128), vm(8, 256), vm(3, 1, 128), vm(sums, 1, 128),
+                        vm(6, 11, 8, 128), vm(64, 128),
+                        pltpu.SemaphoreType.DMA((3, 26)), pltpu.SemaphoreType.DMA((3, 26)), pltpu.SemaphoreType.DMA((sums,)),
                         pltpu.SemaphoreType.DMA((sums,)), pltpu.SemaphoreType.DMA((6,)), pltpu.SemaphoreType.DMA((6,))],
         compiler_params=pltpu.CompilerParams(collective_id=0, has_side_effects=True),
         name="flow",
-    )(w, yld, force, *consts, buf)
+    )(w, yld, force, *consts, counts, xi, vel, mom, new, slots)
 
 def solution(mesh):
     sizes = (mesh.shape["ax"], mesh.shape["circ"], mesh.shape["gap"])
@@ -459,11 +484,8 @@
     def shards(w_old, yield_stress, force, xi, vel, mom, el, new, slots, counts):
         flat = lambda t: t.reshape(256, 128)
         xi, vel, mom = [t.reshape(3, 64, 128) for t in (xi, vel, mom)]
-        buf, dep = pack(xi, vel, mom, new.reshape(64, 128), slots.reshape(6, 8, 128), counts.reshape(6))
-        w, arr = flow(sizes, flat(w_old), flat(yield_stress), flat(force), buf)
-        ax, gap = lax.axis_index("ax"), lax.axis_index("gap")
-        ok = jnp.stack([ax > 0, ax < sizes[0] - 1, ax >= 0, ax >= 0, gap > 0, gap < sizes[2] - 1]).astype(jnp.float32)
-        w_new, kept, arrived = settle(ok, w, xi, vel, mom, el.reshape(64, 128), dep, arr)
+        w, arr, dep = flow(sizes, flat(w_old), flat(yield_stress), flat(force), xi, vel, mom, new.reshape(64, 128), slots.reshape(6, 8, 128), counts.reshape(6))
+        w_new, kept, arrived = settle(sizes, w, xi, vel, mom, el.reshape(64, 128), dep, arr)
         return w_new.reshape(w_old.shape), kept.reshape(1, 1, 1, 9, 8192), arrived.reshape(1, 1, 1, 6, 9, 1024)
 
     spec = lambda n: P("ax", "circ", "gap", *([None] * n))

time: 70.1 us -> 57.9 us (0.83)
  Pallas kernels: 67.9 us -> 56.6 us
    pallas_call x2 -> x1, Pallas kernels: 16.3 us -> 8.72 us  [settle(): pl.pallas_call(functools.partial(settle_kernel, sizes), out_shape=(jax.Sh...]
    pallas_call x1, Pallas kernels: 51.6 us -> 47.9 us  [flow(): pl.pallas_call(functools.partial(flow_kernel, sizes), out_shape=(jax.Shap...]
where the time goes in v3:
time: 57.9 us; the launch traced here: 57.2 us
  Pallas kernels  56.6 us (98%)
  between operations  0.64 us (1%)
    pallas_call x1, Pallas kernels, flow(): pl.pallas_call(functools.partial(flow_kernel, sizes), out_shape=(jax.Shap...  47.9 us
    pallas_call x1, Pallas kernels, settle(): pl.pallas_call(functools.partial(settle_kernel, sizes), out_shape=(jax.Sh...  8.72 us

profile of v3, /device:TPU:1, one launch (start us, length us, event | category | flops | bytes accessed | tf_op | source)
XLA Modules:
  0.0 57.2 jit_solution(9594804942173840059)
XLA Ops:
  0.6 47.9 %flow.1 = (f32[256,128]{1,0:T(8,128)}, f32[6,11,8,128]{3,2,1,0:T(8,128)}, f32[64,128]{1,0:T(8,128)}) custom-call(f32[256,128]{1,0:T(8,128)} %bitcast.19, f32[256,128]{1,0:T(8,128)} %bitcast.20, f32[256,128]{1,0:T(8,128)} %bitcast.21, bf16[256,256]{1,0:T(8,128)(2,1)} %constant.16.clone.lc_ref, bf16[256,256]{1,0:T(8,128)(2,1)} %constant.17.clone.lct_ref, ...), custom_call_target="tpu_custom_call" | custom-call | tf_op jit(solution)/shard_map/flow/pallas_call | solution.py:467
  48.5 8.7 %settle.1 = (f32[256,128]{1,0:T(8,128)}, f32[9,64,128]{2,1,0:T(8,128)}, f32[6,9,8,128]{3,2,1,0:T(8,128)}) custom-call(f32[256,128]{1,0:T(8,128)} %get-tuple-element.9.w_ref, f32[256,128]{1,0:T(8,128)} %constant.23.clone.bary_ref, f32[3,64,128]{2,1,0:T(8,128)} %bitcast.14, f32[3,64,128]{2,1,0:T(8,128)} %bitcast.16, f32[3,64,128]{2,1,0:T(8,128)} %bitcast.18, ...), custom_call_target="tpu_custom_call" | custom-call | tf_op jit(solution)/shard_map/settle/pallas_call | solution.py:147

commit v4 on v3

--- a/solution.py
+++ b/solution.py
@@ -55,6 +55,8 @@
 
     return lax.fori_loop(0, 6, one, jnp.zeros((64, 128), jnp.float32))
 
+STEP = 2
+
 def ladder(x):
     d = [x - np.float32(n) for n in GLL_NODES]
     pre = [None] * 8
@@ -78,7 +80,7 @@
     table_ref[:, 256:384] = high
     lane_g = lax.broadcasted_iota(jnp.int32, (128, 128), 0) // 8
 
-    def sample(ids, x1, x2, x3):
+    def sample(ids, x1, x2, x3, basis_ref, fluid_ref):
         for k, value in enumerate(ladder(x1)):
             basis_ref[0, k * 8:k * 8 + 8, :] = value
         for k, value in enumerate(ladder(x2)):
@@ -118,11 +120,10 @@
         radial = vel[2] * (1.0 - 0.4)
         return [xi[0] + 0.25 * axial, xi[1] + 0.25 * circ, xi[2] + 1.0 * radial, axial, circ, radial]
 
-    @pl.loop(0, 8)
-    def _(block):
+    def stay_block(block, half):
         rows = pl.ds(pl.multiple_of(block * 8, 8), 8)
         xi = [xi_ref[d, rows, :] for d in range(3)]
-        fluid = sample(el_ref[rows, :], *xi)
+        fluid = sample(el_ref[rows, :], *xi, basis_ref.at[half], fluid_ref.at[half])
         stay = 1.0 - dep_ref[rows, :]
         for at, value in enumerate(update(xi, [vel_ref[d, rows, :] for d in range(3)], fluid)):
             kept_ref[at, rows, :] = value * stay
@@ -131,14 +132,23 @@
 
     ax, gap = lax.axis_index("ax"), lax.axis_index("gap")
 
-    @pl.loop(0, 6)
-    def _(row):
+    def arrive_block(row, half):
         absent = ((row == 0) & (ax == 0)) | ((row == 1) & (ax == sizes[0] - 1)) | ((row == 4) & (gap == 0)) | ((row == 5) & (gap == sizes[2] - 1))
         state = [arr_ref[row, d] for d in range(11)]
-        fluid = sample(state[9].astype(jnp.int32), *state[0:3])
+        fluid = sample(state[9].astype(jnp.int32), *state[0:3], basis_ref.at[half], fluid_ref.at[half])
         live = state[10] * jnp.where(absent, 0.0, 1.0)
         for at, value in enumerate(update(state[0:3], state[3:6], fluid) + state[6:9]):
             arrived_ref[row, at] = value * live
+
+    @pl.loop(0, 8 // STEP)
+    def _(block):
+        for half in range(STEP):
+            stay_block(block * STEP + half, half)
+
+    @pl.loop(0, 6 // STEP)
+    def _(row):
+        for half in range(STEP):
+            arrive_block(row * STEP + half, half)
 
 def settle(sizes, w, xi, vel, mom, el, dep, arr):
     b = bary_weights()
@@ -149,7 +159,7 @@
         out_shape=(jax.ShapeDtypeStruct((256, 128), jnp.float32), jax.ShapeDtypeStruct((9, 64, 128), jnp.float32), jax.ShapeDtypeStruct((6, 9, 8, 128), jnp.float32)),
         in_specs=[pl.BlockSpec(memory_space=pltpu.VMEM)] * 8,
         out_specs=(pl.BlockSpec(memory_space=pltpu.VMEM),) * 3,
-        scratch_shapes=[pltpu.VMEM((256, 384), jnp.bfloat16), pltpu.VMEM((4, 64, 128), jnp.float32), pltpu.VMEM((8, 128), jnp.float32)],
+        scratch_shapes=[pltpu.VMEM((256, 384), jnp.bfloat16), pltpu.VMEM((STEP, 4, 64, 128), jnp.float32), pltpu.VMEM((STEP, 8, 128), jnp.float32)],
         name="settle",
     )(w, bary, xi, vel, mom, el, dep, arr)
 
@@ -237,9 +247,14 @@
         out[7 - i] = a - b
     return jnp.concatenate(out, axis=0)
 
-def flow_kernel(sizes, w_ref, yield_ref, force_ref, lc_ref, lct_ref, rg_ref, rgt_ref, small_ref, ends_ref, spread_ref, counts_ref, xi_ref, vel_ref, mom_ref, new_ref, slots_ref,
-                out_ref, arr_ref, dep_ref, v_ref, f_ref, z_ref, quad_ref, stiff_ref, edge_c, edge_e, edge_g, got_a, got_c, got_e, got_g, pair_ref, sum_ref, got_sum, buf_ref, id_ref,
-                send_sem, recv_sem, sum_send, sum_recv, mig_send, mig_recv):
+def flow_kernel(sizes, *refs):
+    sources, (out_ref, arr_ref, dep_ref), held, rest = refs[0:16], refs[16:19], refs[19:35], refs[35:]
+    small_ref, w_ref, force_ref, yield_ref, lc_ref, rg_ref, ends_ref, spread_ref, slots_ref, counts_ref, xi_ref, vel_ref, mom_ref, new_ref, lct_ref, rgt_ref = held
+    (v_ref, f_ref, z_ref, quad_ref, stiff_ref, edge_c, edge_e, edge_g, got_a, got_c, got_e, got_g, pair_ref, sum_ref, got_sum, buf_ref, id_ref,
+     send_sem, recv_sem, sum_send, sum_recv, mig_send, mig_recv, load_sem) = rest
+    loads = [pltpu.make_async_copy(source, mine, load_sem.at[i]) for i, (source, mine) in enumerate(zip(sources, held))]
+    for load in loads:
+        load.start()
     n_ax, n_circ, n_gap = sizes
     d8 = diff_table()
     ax, circ, gap = lax.axis_index("ax"), lax.axis_index("circ"), lax.axis_index("gap")
@@ -255,11 +270,15 @@
         return place
 
     around = [(a, c, g) for a in (0, -1, 1) for c in (0, -1, 1) for g in (0, -1, 1) if (a, c, g) != (0, 0, 0)]
-    peers = [at(*d) for d in around] + [at(da=o) for o in range(2, n_ax - 1)] + [at(dc=o) for o in range(2, n_circ - 1)] + [at(dg=o) for o in range(2, n_gap - 1)]
+    plane = [(a, g) for a in range(n_ax) for g in range(n_gap) if (a, g) != (0, 0)]
+    near = [(a % n_ax, g % n_gap) for a in (0, -1, 1) for g in (0, -1, 1)]
+    peers = [at(*d) for d in around] + [at(dc=o) for o in range(2, n_circ - 1)] + [at(da=o[0], dg=o[1]) for o in plane if o not in near]
     barrier = pltpu.get_barrier_semaphore()
     for peer in peers:
         pl.semaphore_signal(barrier, inc=1, device_id=peer, device_id_type=MESH)
 
+    for load in loads[0:3]:
+        load.wait()
     weights = GLL_WEIGHTS.astype(np.float32)
     quad = jnp.concatenate([small_ref[0] * weights[i] for i in range(8)], axis=0)
     quad_ref[...] = quad
@@ -351,7 +370,6 @@
         pair = jnp.concatenate(thirds(pair) + (jnp.zeros((8, 256), jnp.bfloat16),), axis=0)
         v_ref[k] = (z_ref[k] + mix(pair, spread_ref[...], ((0,), (0,)))) * every(wall)
 
-    id_ref[...] = new_ref[...].astype(jnp.float32)
     fields = [lambda b, ref=ref, d=d: ref[d, b * 8:b * 8 + 8, :] for ref in (xi_ref, vel_ref, mom_ref) for d in range(3)]
     fields.append(lambda b: id_ref[b * 8:b * 8 + 8, :])
     moves = [at(da=1), at(da=-1), at(dc=1), at(dc=-1), at(dg=1), at(dg=-1)]
@@ -368,11 +386,16 @@
 
     stage(0, quad * 0.25 * (4.0 * w_ref[...] + force_ref[...]))
     pl.semaphore_wait(barrier, len(peers))
+    for load in loads[3:7]:
+        load.wait()
     copies = send(0)
     w = w_ref[...]
     slope_a, slope_c, slope_g = along_ax(w, d8), along_circ(w, lc_ref[...]), along_gap(w, rg_ref[...])
     squares = 1.0 + slope_a * slope_a + slope_c * slope_c + slope_g * slope_g
     stiff_ref[...] = quad * 0.25 * (0.05 + yield_ref[...] / jnp.sqrt(squares))
+    for load in loads[7:]:
+        load.wait()
+    id_ref[...] = new_ref[...].astype(jnp.float32)
     pack_rows(0, 3)
     receive(0, copies)
 
@@ -410,11 +433,10 @@
         rows = rows + pltpu.roll(rows, shift, 1)
     line = jnp.sum(jnp.where(sub == part, rows, 0.0), axis=0, keepdims=True)
     slot = 0
-    for step, (name, count) in enumerate((("circ", n_circ), ("ax", n_ax), ("gap", n_gap))):
+    for step, places in enumerate(([at(dc=o) for o in range(1, n_circ)], [at(da=a, dg=g) for a, g in plane])):
         sum_ref[step] = line
         rounds = []
-        for o in range(1, count):
-            place = {"circ": at(dc=o), "ax": at(da=o), "gap": at(dg=o)}[name]
+        for place in places:
             rounds.append(pltpu.make_async_remote_copy(src_ref=sum_ref.at[step], dst_ref=got_sum.at[slot], send_sem=sum_send.at[slot],
                                                        recv_sem=sum_recv.at[slot], device_id=place, device_id_type=MESH))
             slot += 1
@@ -425,8 +447,8 @@
                 copy.wait_send()
         for copy in rounds:
             copy.wait_recv()
-        for o in range(1, count):
-            line = line + got_sum[slot - o]
+        for o in range(len(places)):
+            line = line + got_sum[slot - 1 - o]
         for copy in rounds:
             copy.wait_send()
     m = jnp.sum(jnp.where(sub == part, jnp.broadcast_to(line, (8, 128)), 0.0), axis=1, keepdims=True)
@@ -460,23 +482,25 @@
         copy.wait()
 
 def flow(sizes, w, yld, force, xi, vel, mom, new, slots, counts):
-    consts = field_consts()
+    lc, lct, rg, rgt, small, ends, spread = field_consts()
+    args = (small, w, force, yld, lc, rg, ends, spread, slots, counts, xi, vel, mom, new, lct, rgt)
     vm = lambda *s: pltpu.VMEM(s, jnp.float32)
-    sums = sum(sizes) - 3
+    sums = sizes[1] - 1 + sizes[0] * sizes[2] - 1
     whole = pl.BlockSpec(memory_space=pltpu.VMEM)
+    kept = [pltpu.SMEM(t.shape, t.dtype) if t is counts else pltpu.VMEM(t.shape, t.dtype) for t in args]
     return pl.pallas_call(
         functools.partial(flow_kernel, sizes),
         out_shape=(jax.ShapeDtypeStruct((256, 128), jnp.float32), jax.ShapeDtypeStruct((6, 11, 8, 128), jnp.float32), jax.ShapeDtypeStruct((64, 128), jnp.float32)),
-        in_specs=[whole] * (3 + len(consts)) + [pl.BlockSpec(memory_space=pltpu.SMEM)] + [whole] * 5,
+        in_specs=[pl.BlockSpec(memory_space=pl.ANY)] * 16,
         out_specs=(whole, pl.BlockSpec(memory_space=pl.ANY), whole),
-        scratch_shapes=[vm(3, 256, 128), vm(3, 256, 128), vm(3, 256, 128), vm(256, 128), vm(256, 128), vm(3, 2, 8, 128), vm(3, 4, 1, 128), vm(3, 2, 2, 1, 128),
-                        vm(3, 2, 32, 128), vm(3, 2, 8, 128), vm(3, 4, 1, 128), vm(3, 2, 12, 1, 128), vm(8, 256), vm(3, 1, 128), vm(sums, 1, 128),
+        scratch_shapes=kept + [vm(3, 256, 128), vm(3, 256, 128), vm(3, 256, 128), vm(256, 128), vm(256, 128), vm(3, 2, 8, 128), vm(3, 4, 1, 128), vm(3, 2, 2, 1, 128),
+                        vm(3, 2, 32, 128), vm(3, 2, 8, 128), vm(3, 4, 1, 128), vm(3, 2, 12, 1, 128), vm(8, 256), vm(2, 1, 128), vm(sums, 1, 128),
                         vm(6, 11, 8, 128), vm(64, 128),
                         pltpu.SemaphoreType.DMA((3, 26)), pltpu.SemaphoreType.DMA((3, 26)), pltpu.SemaphoreType.DMA((sums,)),
-                        pltpu.SemaphoreType.DMA((sums,)), pltpu.SemaphoreType.DMA((6,)), pltpu.SemaphoreType.DMA((6,))],
+                        pltpu.SemaphoreType.DMA((sums,)), pltpu.SemaphoreType.DMA((6,)), pltpu.SemaphoreType.DMA((6,)), pltpu.SemaphoreType.DMA((16,))],
         compiler_params=pltpu.CompilerParams(collective_id=0, has_side_effects=True),
         name="flow",
-    )(w, yld, force, *consts, counts, xi, vel, mom, new, slots)
+    )(*args)
 
 def solution(mesh):
     sizes = (mesh.shape["ax"], mesh.shape["circ"], mesh.shape["gap"])

time: 57.9 us -> 54.1 us (0.934)
  Pallas kernels: 56.6 us -> 53.3 us
    pallas_call x1, Pallas kernels: 47.9 us -> 45.9 us  [flow(): pl.pallas_call(functools.partial(flow_kernel, sizes), out_shape=(jax.Shap...]
    pallas_call x1, Pallas kernels: 8.72 us -> 7.38 us  [settle(): pl.pallas_call(functools.partial(settle_kernel, sizes), out_shape=(jax.Sh...]
where the time goes in v4:
time: 54.1 us; the launch traced here: 53.9 us
  Pallas kernels  53.3 us (99%)
  between operations  0.64 us (1%)
    pallas_call x1, Pallas kernels, flow(): pl.pallas_call(functools.partial(flow_kernel, sizes), out_shape=(jax.Shap...  45.9 us
    pallas_call x1, Pallas kernels, settle(): pl.pallas_call(functools.partial(settle_kernel, sizes), out_shape=(jax.Sh...  7.38 us

profile of v4, /device:TPU:1, one launch (start us, length us, event | category | flops | bytes accessed | tf_op | source)
XLA Modules:
  0.0 53.9 jit_solution(11638931642019250230)
XLA Ops:
  0.6 45.9 %flow.1 = (f32[256,128]{1,0:T(8,128)}, f32[6,11,8,128]{3,2,1,0:T(8,128)}, f32[64,128]{1,0:T(8,128)}) custom-call(f32[6,32,128]{2,1,0:T(8,128)} %constant.16.clone.refs_0_, f32[256,128]{1,0:T(8,128)} %bitcast.19, f32[256,128]{1,0:T(8,128)} %bitcast.20, f32[256,128]{1,0:T(8,128)} %bitcast.21, bf16[256,256]{1,0:T(8,128)(2,1)} %constant.17.clone.refs_4_, ...), custom_call_target="tpu_custom_call" | custom-call | tf_op jit(solution)/shard_map/flow/pallas_call | solution.py:491
  46.6 7.4 %settle.1 = (f32[256,128]{1,0:T(8,128)}, f32[9,64,128]{2,1,0:T(8,128)}, f32[6,9,8,128]{3,2,1,0:T(8,128)}) custom-call(f32[256,128]{1,0:T(8,128)} %get-tuple-element.9.w_ref, f32[256,128]{1,0:T(8,128)} %constant.23.clone.bary_ref, f32[3,64,128]{2,1,0:T(8,128)} %bitcast.14, f32[3,64,128]{2,1,0:T(8,128)} %bitcast.16, f32[3,64,128]{2,1,0:T(8,128)} %bitcast.18, ...), custom_call_target="tpu_custom_call" | custom-call | tf_op jit(solution)/shard_map/settle/pallas_call | solution.py:157

commit v5 on v4

--- a/solution.py
+++ b/solution.py
@@ -55,8 +55,6 @@
 
     return lax.fori_loop(0, 6, one, jnp.zeros((64, 128), jnp.float32))
 
-STEP = 2
-
 def ladder(x):
     d = [x - np.float32(n) for n in GLL_NODES]
     pre = [None] * 8
@@ -69,50 +67,77 @@
         suf[k] = suf[k + 1] * d[k + 1]
     return [suf[0]] + [pre[k] * suf[k] for k in range(1, 7)] + [pre[7]]
 
-def settle_kernel(sizes, w_ref, bary_ref, xi_ref, vel_ref, mom_ref, el_ref, dep_ref, arr_ref, w_out, kept_ref, arrived_ref, table_ref, basis_ref, fluid_ref):
-    w = w_ref[...]
-    w_out[...] = w
-    w = w * bary_ref[...]
-    high = w.astype(jnp.bfloat16)
-    low = (w - high.astype(jnp.float32)).astype(jnp.bfloat16)
-    table_ref[:, 0:128] = high
-    table_ref[:, 128:256] = low
-    table_ref[:, 256:384] = high
-    lane_g = lax.broadcasted_iota(jnp.int32, (128, 128), 0) // 8
-
-    def sample(ids, x1, x2, x3, basis_ref, fluid_ref):
-        for k, value in enumerate(ladder(x1)):
-            basis_ref[0, k * 8:k * 8 + 8, :] = value
-        for k, value in enumerate(ladder(x2)):
-            basis_ref[1, k * 8:k * 8 + 8, :] = value
-        for k, value in enumerate(ladder(x3)):
-            rounded = value.astype(jnp.bfloat16).astype(jnp.float32)
-            basis_ref[2, k * 8:k * 8 + 8, :] = rounded
-            basis_ref[3, k * 8:k * 8 + 8, :] = value - rounded
-        circ = lax.shift_right_logical(ids, 4)
-        radial = lax.bitwise_and(ids, 15)
-        for q in range(4):
-            right, weights = [], []
-            for s in (2 * q, 2 * q + 1):
-                mine = lane_g == jnp.broadcast_to(radial[s:s + 1], (128, 128))
-                b_high = jnp.where(mine, jnp.concatenate([basis_ref[2, pl.ds(s, 8, stride=8), :]] * 16, axis=0), 0.0).astype(jnp.bfloat16)
-                b_low = jnp.where(mine, jnp.concatenate([basis_ref[3, pl.ds(s, 8, stride=8), :]] * 16, axis=0), 0.0).astype(jnp.bfloat16)
-                right.append(jnp.concatenate([b_high, b_high, b_low], axis=0))
-                second = basis_ref[1, pl.ds(s, 8, stride=8), :]
-                cc = jnp.broadcast_to(circ[s:s + 1], (8, 128))
-                weights.append([jnp.where(cc == c, second, 0.0) for c in range(4)])
-            values = jnp.dot(table_ref[...], jnp.concatenate(right, axis=1), preferred_element_type=jnp.float32)
-            for h, s in enumerate((2 * q, 2 * q + 1)):
+LATE = 3
+
+def bary_table():
+    b = bary_weights()
+    rows = (b[:, None, None] * np.ones((1, 4, 1)) * b[None, None, :]).reshape(256, 1)
+    return np.ascontiguousarray(rows * np.tile(b, 16)[None, :], dtype=np.float32)
+
+def make_table(table_ref, k, v, bary):
+    v = (v * bary).reshape(16, 2, 8, 128)
+    v = jnp.concatenate([v[:, 0].reshape(128, 128), v[:, 1].reshape(128, 128)], axis=1)
+    high = v.astype(jnp.bfloat16)
+    low = (v - high.astype(jnp.float32)).astype(jnp.bfloat16)
+    table_ref[k, :, 0:256] = high
+    table_ref[k, :, 256:512] = low
+    table_ref[k, :, 512:768] = high
+
+def sample(table_ref, first, count, ids, points, basis_ref, put):
+    for d in range(2):
+        for k, value in enumerate(ladder(points[d])):
+            basis_ref[d, k * 8:k * 8 + 8, :] = value
+    for k, value in enumerate(ladder(points[2])):
+        rounded = value.astype(jnp.bfloat16).astype(jnp.float32)
+        basis_ref[2, k * 8:k * 8 + 8, :] = rounded
+        basis_ref[3, k * 8:k * 8 + 8, :] = value - rounded
+    second_half = jnp.where(lax.broadcasted_iota(jnp.int32, (16, 128), 0) >= 8, 1.0, 0.0)
+    zero = jnp.zeros((16, 128), jnp.bfloat16)
+    circ = lax.shift_right_logical(ids, 5)
+    radial = lax.bitwise_and(ids, 31).astype(jnp.float32)
+    table = table_ref[first:first + count].reshape(count * 128, 768)
+    for q in range(4):
+        right, weights = [], []
+        for s in (2 * q, 2 * q + 1):
+            mine = (jnp.broadcast_to(radial[s:s + 1], (16, 128)) - second_half).astype(jnp.bfloat16)
+            high16 = jnp.concatenate([basis_ref[2, pl.ds(s, 8, stride=8), :]] * 2, axis=0).astype(jnp.bfloat16)
+            low16 = jnp.concatenate([basis_ref[3, pl.ds(s, 8, stride=8), :]] * 2, axis=0).astype(jnp.bfloat16)
+            same = [mine == jnp.bfloat16(2 * t) for t in range(16)]
+            b_high = jnp.concatenate([jnp.where(m, high16, zero) for m in same], axis=0)
+            b_low = jnp.concatenate([jnp.where(m, low16, zero) for m in same], axis=0)
+            right.append(jnp.concatenate([b_high, b_high, b_low], axis=0))
+            second = basis_ref[1, pl.ds(s, 8, stride=8), :]
+            cc = jnp.broadcast_to(circ[s:s + 1], (8, 128))
+            weights.append([jnp.where(cc == c, second, 0.0) for c in range(2)])
+        values = jnp.dot(table, jnp.concatenate(right, axis=1), preferred_element_type=jnp.float32)
+        for h, s in enumerate((2 * q, 2 * q + 1)):
+            for n in range(count):
                 total = None
                 for i in range(8):
                     line = None
-                    for c in range(4):
-                        term = values[i * 32 + c * 8:i * 32 + c * 8 + 8, h * 128:h * 128 + 128] * weights[h][c]
+                    for c in range(2):
+                        at = n * 128 + i * 16 + c * 8
+                        term = values[at:at + 8, h * 128:h * 128 + 128] * weights[h][c]
                         line = term if line is None else line + term
                     line = line * jnp.broadcast_to(basis_ref[0, i * 8 + s:i * 8 + s + 1, :], (8, 128))
                     total = line if total is None else total + line
-                fluid_ref[s:s + 1, :] = jnp.sum(total, axis=0, keepdims=True)
-        return fluid_ref[...]
+                put(first + n, s, jnp.sum(total, axis=0, keepdims=True))
+
+def finish_kernel(sizes, w_ref, bary_ref, fluid_ref, xi_ref, vel_ref, mom_ref, dep_ref, arr_ref, w_out, kept_ref, arrived_ref, table_ref, basis_ref, late_ref):
+    w_out[...] = w_ref[...]
+    make_table(table_ref, 0, w_ref[...], bary_ref[...])
+
+    def keeper(row):
+        def put(k, s, value):
+            late_ref[row, s:s + 1, :] = value
+
+        return put
+
+    for row in range(LATE):
+        at = 6 - LATE + row
+        sample(table_ref, 0, 1, arr_ref[at, 9].astype(jnp.int32), [arr_ref[at, d] for d in range(3)], basis_ref.at[row], keeper(row))
+    ax, gap = lax.axis_index("ax"), lax.axis_index("gap")
+    absent = [ax == 0, ax == sizes[0] - 1, None, None, gap == 0, gap == sizes[2] - 1]
 
     def update(xi, vel, fluid):
         axial = vel[0] + 0.4 * (fluid - vel[0])
@@ -120,48 +145,27 @@
         radial = vel[2] * (1.0 - 0.4)
         return [xi[0] + 0.25 * axial, xi[1] + 0.25 * circ, xi[2] + 1.0 * radial, axial, circ, radial]
 
-    def stay_block(block, half):
-        rows = pl.ds(pl.multiple_of(block * 8, 8), 8)
-        xi = [xi_ref[d, rows, :] for d in range(3)]
-        fluid = sample(el_ref[rows, :], *xi, basis_ref.at[half], fluid_ref.at[half])
-        stay = 1.0 - dep_ref[rows, :]
-        for at, value in enumerate(update(xi, [vel_ref[d, rows, :] for d in range(3)], fluid)):
-            kept_ref[at, rows, :] = value * stay
-        for d in range(3):
-            kept_ref[6 + d, rows, :] = mom_ref[d, rows, :] * stay
-
-    ax, gap = lax.axis_index("ax"), lax.axis_index("gap")
-
-    def arrive_block(row, half):
-        absent = ((row == 0) & (ax == 0)) | ((row == 1) & (ax == sizes[0] - 1)) | ((row == 4) & (gap == 0)) | ((row == 5) & (gap == sizes[2] - 1))
+    stay = 1.0 - dep_ref[...]
+    state = update([xi_ref[d] for d in range(3)], [vel_ref[d] for d in range(3)], fluid_ref[0:64]) + [mom_ref[d] for d in range(3)]
+    for at, value in enumerate(state):
+        kept_ref[at] = value * stay
+    for row in range(6):
         state = [arr_ref[row, d] for d in range(11)]
-        fluid = sample(state[9].astype(jnp.int32), *state[0:3], basis_ref.at[half], fluid_ref.at[half])
-        live = state[10] * jnp.where(absent, 0.0, 1.0)
+        live = state[10] if absent[row] is None else state[10] * jnp.where(absent[row], 0.0, 1.0)
+        fluid = fluid_ref[64 + 8 * row:72 + 8 * row] if row < 6 - LATE else late_ref[row - 6 + LATE]
         for at, value in enumerate(update(state[0:3], state[3:6], fluid) + state[6:9]):
             arrived_ref[row, at] = value * live
 
-    @pl.loop(0, 8 // STEP)
-    def _(block):
-        for half in range(STEP):
-            stay_block(block * STEP + half, half)
-
-    @pl.loop(0, 6 // STEP)
-    def _(row):
-        for half in range(STEP):
-            arrive_block(row * STEP + half, half)
-
-def settle(sizes, w, xi, vel, mom, el, dep, arr):
-    b = bary_weights()
-    rows = (b[:, None, None] * np.ones((1, 4, 1)) * b[None, None, :]).reshape(256, 1)
-    bary = np.ascontiguousarray(rows * np.tile(b, 16)[None, :], dtype=np.float32)
+def finish(sizes, w, bary, fluid, xi, vel, mom, dep, arr):
     return pl.pallas_call(
-        functools.partial(settle_kernel, sizes),
+        functools.partial(finish_kernel, sizes),
         out_shape=(jax.ShapeDtypeStruct((256, 128), jnp.float32), jax.ShapeDtypeStruct((9, 64, 128), jnp.float32), jax.ShapeDtypeStruct((6, 9, 8, 128), jnp.float32)),
         in_specs=[pl.BlockSpec(memory_space=pltpu.VMEM)] * 8,
         out_specs=(pl.BlockSpec(memory_space=pltpu.VMEM),) * 3,
-        scratch_shapes=[pltpu.VMEM((256, 384), jnp.bfloat16), pltpu.VMEM((STEP, 4, 64, 128), jnp.float32), pltpu.VMEM((STEP, 8, 128), jnp.float32)],
-        name="settle",
-    )(w, bary, xi, vel, mom, el, dep, arr)
+        scratch_shapes=[pltpu.VMEM((1, 128, 768), jnp.bfloat16), pltpu.VMEM((LATE, 4, 64, 128), jnp.float32), pltpu.VMEM((LATE, 8, 128), jnp.float32)],
+        name="finish",
+    )(w, bary, fluid, xi, vel, mom, dep, arr)
+
 
 def diff_table():
     b = bary_weights()
@@ -248,10 +252,10 @@
     return jnp.concatenate(out, axis=0)
 
 def flow_kernel(sizes, *refs):
-    sources, (out_ref, arr_ref, dep_ref), held, rest = refs[0:16], refs[16:19], refs[19:35], refs[35:]
-    small_ref, w_ref, force_ref, yield_ref, lc_ref, rg_ref, ends_ref, spread_ref, slots_ref, counts_ref, xi_ref, vel_ref, mom_ref, new_ref, lct_ref, rgt_ref = held
-    (v_ref, f_ref, z_ref, quad_ref, stiff_ref, edge_c, edge_e, edge_g, got_a, got_c, got_e, got_g, pair_ref, sum_ref, got_sum, buf_ref, id_ref,
-     send_sem, recv_sem, sum_send, sum_recv, mig_send, mig_recv, load_sem) = rest
+    sources, (out_ref, arr_out, dep_ref, fluid_ref), held, rest = refs[0:18], refs[18:22], refs[22:40], refs[40:]
+    small_ref, w_ref, force_ref, yield_ref, lc_ref, rg_ref, ends_ref, spread_ref, slots_ref, counts_ref, xi_ref, vel_ref, mom_ref, new_ref, lct_ref, rgt_ref, bary_ref, el_ref = held
+    (v_ref, f_ref, z_ref, quad_ref, stiff_ref, edge_c, edge_e, edge_g, got_a, got_c, got_e, got_g, pair_ref, sum_ref, got_sum, buf_ref, id_ref, arr_ref, table_ref, basis_ref, part_ref,
+     send_sem, recv_sem, sum_send, sum_recv, mig_send, mig_recv, load_sem, keep_sem) = rest
     loads = [pltpu.make_async_copy(source, mine, load_sem.at[i]) for i, (source, mine) in enumerate(zip(sources, held))]
     for load in loads:
         load.start()
@@ -399,6 +403,25 @@
     pack_rows(0, 3)
     receive(0, copies)
 
+    def keeper(base, half):
+        def put(k, s, value):
+            part_ref[k, base, s:s + 1, :] = value
+
+        return put
+
+    def sample_kept(first, count, block, half):
+        rows = pl.ds(pl.multiple_of(block * 8, 8), 8)
+        sample(table_ref, first, count, el_ref[rows, :], [xi_ref[d, rows, :] for d in range(3)], basis_ref.at[half], keeper(block, half))
+
+    def sample_arrived(first, count, row, half):
+        sample(table_ref, first, count, arr_ref[row, 9].astype(jnp.int32), [arr_ref[row, d] for d in range(3)], basis_ref.at[half], keeper(row + 8, half))
+
+    def sample_pairs(first, count):
+        @pl.loop(0, 3)
+        def _(two):
+            for half in range(2):
+                sample_kept(first, count, two * 2 + half, half)
+
     def total(x):
         return jnp.sum(x.reshape(32, 8, 128), axis=0)
 
@@ -417,8 +440,11 @@
         sums.append(total(quad_ref[...] * square + stiff * (slope_a * slope_a + slope_c * slope_c + slope_g * slope_g)))
         if k == 0:
             pack_rows(3, 6)
+            dep_ref[...] = departed_flags(slots_ref, counts_ref)
+            make_table(table_ref, 0, v_ref[0], bary_ref[...])
         if k == 1:
-            dep_ref[...] = departed_flags(slots_ref, counts_ref)
+            make_table(table_ref, 1, v_ref[1], bary_ref[...])
+            sample_pairs(0, 2)
         if k < 2:
             for copy in sent:
                 copy.wait_send()
@@ -432,6 +458,7 @@
     for shift in (64, 32, 16):
         rows = rows + pltpu.roll(rows, shift, 1)
     line = jnp.sum(jnp.where(sub == part, rows, 0.0), axis=0, keepdims=True)
+    keep = pltpu.make_async_copy(arr_ref, arr_out, keep_sem)
     slot = 0
     for step, places in enumerate(([at(dc=o) for o in range(1, n_circ)], [at(da=a, dg=g) for a, g in plane])):
         sum_ref[step] = line
@@ -445,6 +472,17 @@
         if step == 0:
             for copy in copies:
                 copy.wait_send()
+            make_table(table_ref, 2, v_ref[2], bary_ref[...])
+            sample_pairs(2, 1)
+            sample_kept(0, 3, 6, 0)
+        else:
+            for copy in moving:
+                copy.wait()
+            keep.start()
+            sample_arrived(0, 3, 0, 0)
+            sample_arrived(0, 3, 1, 1)
+            sample_kept(0, 3, 7, 0)
+            sample_arrived(0, 3, 2, 1)
         for copy in rounds:
             copy.wait_recv()
         for o in range(len(places)):
@@ -478,26 +516,29 @@
     x1 = scale * scale * (-(c2 + a2 * (c1 + b1 * a0)))
     x2 = scale * scale * scale * (a2 * c2)
     out_ref[...] = x0 * v_ref[0] + x1 * v_ref[1] + x2 * v_ref[2]
-    for copy in moving:
-        copy.wait()
-
-def flow(sizes, w, yld, force, xi, vel, mom, new, slots, counts):
+    for base in range(14 - LATE):
+        fluid_ref[base * 8:base * 8 + 8, :] = x0 * part_ref[0, base] + x1 * part_ref[1, base] + x2 * part_ref[2, base]
+    keep.wait()
+
+def flow(sizes, w, yld, force, xi, vel, mom, new, slots, counts, el):
+    bary = bary_table()
     lc, lct, rg, rgt, small, ends, spread = field_consts()
-    args = (small, w, force, yld, lc, rg, ends, spread, slots, counts, xi, vel, mom, new, lct, rgt)
+    args = (small, w, force, yld, lc, rg, ends, spread, slots, counts, xi, vel, mom, new, lct, rgt, bary, el)
     vm = lambda *s: pltpu.VMEM(s, jnp.float32)
     sums = sizes[1] - 1 + sizes[0] * sizes[2] - 1
     whole = pl.BlockSpec(memory_space=pltpu.VMEM)
     kept = [pltpu.SMEM(t.shape, t.dtype) if t is counts else pltpu.VMEM(t.shape, t.dtype) for t in args]
     return pl.pallas_call(
         functools.partial(flow_kernel, sizes),
-        out_shape=(jax.ShapeDtypeStruct((256, 128), jnp.float32), jax.ShapeDtypeStruct((6, 11, 8, 128), jnp.float32), jax.ShapeDtypeStruct((64, 128), jnp.float32)),
-        in_specs=[pl.BlockSpec(memory_space=pl.ANY)] * 16,
-        out_specs=(whole, pl.BlockSpec(memory_space=pl.ANY), whole),
+        out_shape=(jax.ShapeDtypeStruct((256, 128), jnp.float32), jax.ShapeDtypeStruct((6, 11, 8, 128), jnp.float32), jax.ShapeDtypeStruct((64, 128), jnp.float32),
+                   jax.ShapeDtypeStruct((112 - 8 * LATE, 128), jnp.float32)),
+        in_specs=[pl.BlockSpec(memory_space=pl.ANY)] * 18,
+        out_specs=(whole, pl.BlockSpec(memory_space=pl.ANY), whole, whole),
         scratch_shapes=kept + [vm(3, 256, 128), vm(3, 256, 128), vm(3, 256, 128), vm(256, 128), vm(256, 128), vm(3, 2, 8, 128), vm(3, 4, 1, 128), vm(3, 2, 2, 1, 128),
                         vm(3, 2, 32, 128), vm(3, 2, 8, 128), vm(3, 4, 1, 128), vm(3, 2, 12, 1, 128), vm(8, 256), vm(2, 1, 128), vm(sums, 1, 128),
-                        vm(6, 11, 8, 128), vm(64, 128),
+                        vm(6, 11, 8, 128), vm(64, 128), vm(6, 11, 8, 128), pltpu.VMEM((3, 128, 768), jnp.bfloat16), vm(2, 4, 64, 128), vm(3, 14, 8, 128),
                         pltpu.SemaphoreType.DMA((3, 26)), pltpu.SemaphoreType.DMA((3, 26)), pltpu.SemaphoreType.DMA((sums,)),
-                        pltpu.SemaphoreType.DMA((sums,)), pltpu.SemaphoreType.DMA((6,)), pltpu.SemaphoreType.DMA((6,)), pltpu.SemaphoreType.DMA((16,))],
+                        pltpu.SemaphoreType.DMA((sums,)), pltpu.SemaphoreType.DMA((6,)), pltpu.SemaphoreType.DMA((6,)), pltpu.SemaphoreType.DMA((18,)), pltpu.SemaphoreType.DMA],
         compiler_params=pltpu.CompilerParams(collective_id=0, has_side_effects=True),
         name="flow",
     )(*args)
@@ -508,8 +549,8 @@
     def shards(w_old, yield_stress, force, xi, vel, mom, el, new, slots, counts):
         flat = lambda t: t.reshape(256, 128)
         xi, vel, mom = [t.reshape(3, 64, 128) for t in (xi, vel, mom)]
-        w, arr, dep = flow(sizes, flat(w_old), flat(yield_stress), flat(force), xi, vel, mom, new.reshape(64, 128), slots.reshape(6, 8, 128), counts.reshape(6))
-        w_new, kept, arrived = settle(sizes, w, xi, vel, mom, el.reshape(64, 128), dep, arr)
+        w, arr, dep, fluid = flow(sizes, flat(w_old), flat(yield_stress), flat(force), xi, vel, mom, new.reshape(64, 128), slots.reshape(6, 8, 128), counts.reshape(6), el.reshape(64, 128))
+        w_new, kept, arrived = finish(sizes, w, bary_table(), fluid, xi, vel, mom, dep, arr)
         return w_new.reshape(w_old.shape), kept.reshape(1, 1, 1, 9, 8192), arrived.reshape(1, 1, 1, 6, 9, 1024)
 
     spec = lambda n: P("ax", "circ", "gap", *([None] * n))

time: 54.1 us -> 49.5 us (0.915)
  Pallas kernels: 53.3 us -> 48.7 us
    pallas_call x1, Pallas kernels: 7.38 us -> 2.84 us  [finish(): pl.pallas_call(functools.partial(finish_kernel, sizes), out_shape=(jax.Sh...]
where the time goes in v5:
time: 49.5 us; the launch traced here: 49.4 us
  Pallas kernels  48.7 us (98%)
  between operations  0.64 us (1%)
    pallas_call x1, Pallas kernels, flow(): pl.pallas_call(functools.partial(flow_kernel, sizes), out_shape=(jax.Shap...  45.9 us
    pallas_call x1, Pallas kernels, finish(): pl.pallas_call(functools.partial(finish_kernel, sizes), out_shape=(jax.Sh...  2.84 us

profile of v5, /device:TPU:1, one launch (start us, length us, event | category | flops | bytes accessed | tf_op | source)
XLA Modules:
  0.0 49.4 jit_solution(3328210450080743940)
XLA Ops:
  0.6 45.9 %flow.1 = (f32[256,128]{1,0:T(8,128)}, f32[6,11,8,128]{3,2,1,0:T(8,128)}, f32[64,128]{1,0:T(8,128)}, f32[88,128]{1,0:T(8,128)}) custom-call(f32[6,32,128]{2,1,0:T(8,128)} %constant.16.clone.refs_0_, f32[256,128]{1,0:T(8,128)} %bitcast.19, f32[256,128]{1,0:T(8,128)} %bitcast.20, f32[256,128]{1,0:T(8,128)} %bitcast.21, ...), custom_call_target="tpu_custom_call" | custom-call | tf_op jit(solution)/shard_map/flow/pallas_call | solution.py:531
  46.5 2.8 %finish.1 = (f32[256,128]{1,0:T(8,128)}, f32[9,64,128]{2,1,0:T(8,128)}, f32[6,9,8,128]{3,2,1,0:T(8,128)}) custom-call(f32[256,128]{1,0:T(8,128)} %get-tuple-element.10.w_ref, f32[256,128]{1,0:T(8,128)} %constant.23.clone.refs_16_.bary_ref, f32[88,128]{1,0:T(8,128)} %get-tuple-element.11.fluid_ref, f32[3,64,128]{2,1,0:T(8,128)} %bitcast.14, ...), custom_call_target="tpu_custom_call" | custom-call | tf_op jit(solution)/shard_map/finish/pallas_call | solution.py:160

commit v6 on v5

--- a/solution.py
+++ b/solution.py
@@ -67,7 +67,7 @@
         suf[k] = suf[k + 1] * d[k + 1]
     return [suf[0]] + [pre[k] * suf[k] for k in range(1, 7)] + [pre[7]]
 
-LATE = 3
+LATE = 2
 
 def bary_table():
     b = bary_weights()
@@ -253,7 +253,7 @@
 
 def flow_kernel(sizes, *refs):
     sources, (out_ref, arr_out, dep_ref, fluid_ref), held, rest = refs[0:18], refs[18:22], refs[22:40], refs[40:]
-    small_ref, w_ref, force_ref, yield_ref, lc_ref, rg_ref, ends_ref, spread_ref, slots_ref, counts_ref, xi_ref, vel_ref, mom_ref, new_ref, lct_ref, rgt_ref, bary_ref, el_ref = held
+    small_ref, w_ref, force_ref, ends_ref, yield_ref, lc_ref, rg_ref, spread_ref, slots_ref, counts_ref, xi_ref, vel_ref, mom_ref, new_ref, lct_ref, rgt_ref, bary_ref, el_ref = held
     (v_ref, f_ref, z_ref, quad_ref, stiff_ref, edge_c, edge_e, edge_g, got_a, got_c, got_e, got_g, pair_ref, sum_ref, got_sum, buf_ref, id_ref, arr_ref, table_ref, basis_ref, part_ref,
      send_sem, recv_sem, sum_send, sum_recv, mig_send, mig_recv, load_sem, keep_sem) = rest
     loads = [pltpu.make_async_copy(source, mine, load_sem.at[i]) for i, (source, mine) in enumerate(zip(sources, held))]
@@ -277,11 +277,14 @@
     plane = [(a, g) for a in range(n_ax) for g in range(n_gap) if (a, g) != (0, 0)]
     near = [(a % n_ax, g % n_gap) for a in (0, -1, 1) for g in (0, -1, 1)]
     peers = [at(*d) for d in around] + [at(dc=o) for o in range(2, n_circ - 1)] + [at(da=o[0], dg=o[1]) for o in plane if o not in near]
+    hops = lambda d, n: min(d, n - d)
+    far_circ = sorted(range(1, n_circ), key=lambda o: -hops(o, n_circ))
+    far_plane = sorted(plane, key=lambda o: -(hops(o[0], n_ax) + hops(o[1], n_gap)))
     barrier = pltpu.get_barrier_semaphore()
     for peer in peers:
         pl.semaphore_signal(barrier, inc=1, device_id=peer, device_id_type=MESH)
 
-    for load in loads[0:3]:
+    for load in loads[0:4]:
         load.wait()
     weights = GLL_WEIGHTS.astype(np.float32)
     quad = jnp.concatenate([small_ref[0] * weights[i] for i in range(8)], axis=0)
@@ -316,16 +319,14 @@
         edge_c[k, 1] = f_ref[k, pl.ds(31, 8, stride=32), :]
         for e, at_row in enumerate((0, 31, 224, 255)):
             edge_e[k, e] = f_ref[k, at_row:at_row + 1, :]
-
-    def send(k):
+        return mix(ends_ref[...], jnp.concatenate(thirds(f), axis=1), ((1,), (1,)))
+
+    def send(k, faces):
         copies = [remote(edge_e.at[k, e], got_e.at[k, 3 - e], k, 4 + e, at(da=1 if e >= 2 else -1, dc=1 if e % 2 else -1)) for e in range(4)]
         copies += [remote(edge_c.at[k, 0], got_c.at[k, 1], k, 2, at(dc=-1)),
                    remote(edge_c.at[k, 1], got_c.at[k, 0], k, 3, at(dc=1)),
                    remote(f_ref.at[k, 0:32], got_a.at[k, 1], k, 0, at(da=-1)),
                    remote(f_ref.at[k, 224:256], got_a.at[k, 0], k, 1, at(da=1))]
-        for copy in copies:
-            copy.start()
-        faces = mix(ends_ref[...], jnp.concatenate(thirds(f_ref[k]), axis=1), ((1,), (1,)))
         for s in range(2):
             for h in range(2):
                 edge_g[k, s, h] = faces[s:s + 1, h * 128:h * 128 + 128]
@@ -343,7 +344,7 @@
             for c in (0, -1, 1):
                 slot = {0: 0, 1: 1, -1: 2}[c]
                 later.append(remote(edge_g.at[k, s], got_g.at[k, 1 - s, 2 * slot:2 * slot + 2], k, t + slot, at(dc=c, dg=dg)))
-        for copy in later:
+        for copy in later + copies:
             copy.start()
         return copies + later
 
@@ -388,11 +389,11 @@
         for copy in moving[first:last]:
             copy.start()
 
-    stage(0, quad * 0.25 * (4.0 * w_ref[...] + force_ref[...]))
+    faces = stage(0, quad * 0.25 * (4.0 * w_ref[...] + force_ref[...]))
     pl.semaphore_wait(barrier, len(peers))
-    for load in loads[3:7]:
+    for load in loads[4:7]:
         load.wait()
-    copies = send(0)
+    copies = send(0, faces)
     w = w_ref[...]
     slope_a, slope_c, slope_g = along_ax(w, d8), along_circ(w, lc_ref[...]), along_gap(w, rg_ref[...])
     squares = 1.0 + slope_a * slope_a + slope_c * slope_c + slope_g * slope_g
@@ -401,6 +402,7 @@
         load.wait()
     id_ref[...] = new_ref[...].astype(jnp.float32)
     pack_rows(0, 3)
+    dep_ref[...] = departed_flags(slots_ref, counts_ref)
     receive(0, copies)
 
     def keeper(base, half):
@@ -433,15 +435,16 @@
         if k < 2:
             image = quad_ref[...] * v + along_ax(stiff * slope_a, d8.T)
             image = image + along_circ(stiff * slope_c, lct_ref[...]) + along_gap(stiff * slope_g, rgt_ref[...])
-            stage(k + 1, image)
-            sent, copies = copies, send(k + 1)
+            faces = stage(k + 1, image)
+            sent, copies = copies, send(k + 1, faces)
         square = v * v
         sums.append(total(jnp.concatenate([square[i * 32:i * 32 + 32] * (share * ax_share[i]) for i in range(8)], axis=0)))
         sums.append(total(quad_ref[...] * square + stiff * (slope_a * slope_a + slope_c * slope_c + slope_g * slope_g)))
         if k == 0:
             pack_rows(3, 6)
-            dep_ref[...] = departed_flags(slots_ref, counts_ref)
             make_table(table_ref, 0, v_ref[0], bary_ref[...])
+            sample_kept(0, 1, 6, 0)
+            sample_kept(0, 1, 7, 1)
         if k == 1:
             make_table(table_ref, 1, v_ref[1], bary_ref[...])
             sample_pairs(0, 2)
@@ -460,7 +463,7 @@
     line = jnp.sum(jnp.where(sub == part, rows, 0.0), axis=0, keepdims=True)
     keep = pltpu.make_async_copy(arr_ref, arr_out, keep_sem)
     slot = 0
-    for step, places in enumerate(([at(dc=o) for o in range(1, n_circ)], [at(da=a, dg=g) for a, g in plane])):
+    for step, places in enumerate(([at(dc=o) for o in far_circ], [at(da=a, dg=g) for a, g in far_plane])):
         sum_ref[step] = line
         rounds = []
         for place in places:
@@ -474,15 +477,16 @@
                 copy.wait_send()
             make_table(table_ref, 2, v_ref[2], bary_ref[...])
             sample_pairs(2, 1)
-            sample_kept(0, 3, 6, 0)
+            sample_kept(1, 2, 6, 0)
         else:
             for copy in moving:
                 copy.wait()
             keep.start()
             sample_arrived(0, 3, 0, 0)
             sample_arrived(0, 3, 1, 1)
-            sample_kept(0, 3, 7, 0)
-            sample_arrived(0, 3, 2, 1)
+            sample_arrived(0, 3, 2, 0)
+            sample_arrived(0, 3, 3, 1)
+            sample_kept(1, 2, 7, 0)
         for copy in rounds:
             copy.wait_recv()
         for o in range(len(places)):
@@ -523,7 +527,7 @@
 def flow(sizes, w, yld, force, xi, vel, mom, new, slots, counts, el):
     bary = bary_table()
     lc, lct, rg, rgt, small, ends, spread = field_consts()
-    args = (small, w, force, yld, lc, rg, ends, spread, slots, counts, xi, vel, mom, new, lct, rgt, bary, el)
+    args = (small, w, force, ends, yld, lc, rg, spread, slots, counts, xi, vel, mom, new, lct, rgt, bary, el)
     vm = lambda *s: pltpu.VMEM(s, jnp.float32)
     sums = sizes[1] - 1 + sizes[0] * sizes[2] - 1
     whole = pl.BlockSpec(memory_space=pltpu.VMEM)

time: 49.5 us -> 49 us (0.990)
  Pallas kernels: 48.7 us -> 48.2 us
where the time goes in v6:
time: 49 us; the launch traced here: 48.8 us
  Pallas kernels  48.2 us (98%)
  between operations  0.64 us (1%)
    pallas_call x1, Pallas kernels, flow(): pl.pallas_call(functools.partial(flow_kernel, sizes), out_shape=(jax.Shap...  45.5 us
    pallas_call x1, Pallas kernels, finish(): pl.pallas_call(functools.partial(finish_kernel, sizes), out_shape=(jax.Sh...  2.65 us

profile of v6, /device:TPU:1, one launch (start us, length us, event | category | flops | bytes accessed | tf_op | source)
XLA Modules:
  0.0 48.8 jit_solution(9516074749232758658)
XLA Ops:
  0.6 45.5 %flow.1 = (f32[256,128]{1,0:T(8,128)}, f32[6,11,8,128]{3,2,1,0:T(8,128)}, f32[64,128]{1,0:T(8,128)}, f32[96,128]{1,0:T(8,128)}) custom-call(f32[6,32,128]{2,1,0:T(8,128)} %constant.16.clone.refs_0_, f32[256,128]{1,0:T(8,128)} %bitcast.19, f32[256,128]{1,0:T(8,128)} %bitcast.20, bf16[8,384]{1,0:T(8,128)(2,1)} %constant.17.clone.refs_3_, f32[256,128]{1,0:T(8,128)} %bitcast.21, ...), custom_call_target="tpu_custom_call" | custom-call | tf_op jit(solution)/shard_map/flow/pallas_call | solution.py:535
  46.2 2.6 %finish.1 = (f32[256,128]{1,0:T(8,128)}, f32[9,64,128]{2,1,0:T(8,128)}, f32[6,9,8,128]{3,2,1,0:T(8,128)}) custom-call(f32[256,128]{1,0:T(8,128)} %get-tuple-element.10.w_ref, f32[256,128]{1,0:T(8,128)} %constant.23.clone.refs_16_.bary_ref, f32[96,128]{1,0:T(8,128)} %get-tuple-element.11.fluid_ref, f32[3,64,128]{2,1,0:T(8,128)} %bitcast.14, ...), custom_call_target="tpu_custom_call" | custom-call | tf_op jit(solution)/shard_map/finish/pallas_call | solution.py:160

commit v7 on v6

--- a/solution.py
+++ b/solution.py
@@ -123,9 +123,13 @@
                     total = line if total is None else total + line
                 put(first + n, s, jnp.sum(total, axis=0, keepdims=True))
 
-def finish_kernel(sizes, w_ref, bary_ref, fluid_ref, xi_ref, vel_ref, mom_ref, dep_ref, arr_ref, w_out, kept_ref, arrived_ref, table_ref, basis_ref, late_ref):
-    w_out[...] = w_ref[...]
-    make_table(table_ref, 0, w_ref[...], bary_ref[...])
+def finish_kernel(sizes, *refs):
+    sources, outs, held, (kept_ref, arrived_ref, table_ref, basis_ref, late_ref, load_sem, save_sem) = refs[0:8], refs[8:11], refs[11:19], refs[19:]
+    fluid_ref, vel_ref, xi_ref, mom_ref, dep_ref, w_ref, bary_ref, arr_ref = held
+    loads = [pltpu.make_async_copy(source, mine, load_sem.at[i]) for i, (source, mine) in enumerate(zip(sources, held))]
+    for load in loads:
+        load.start()
+    saves = [pltpu.make_async_copy(mine, out, save_sem.at[i]) for i, (mine, out) in enumerate(zip((w_ref, kept_ref, arrived_ref), outs))]
 
     def keeper(row):
         def put(k, s, value):
@@ -133,9 +137,6 @@
 
         return put
 
-    for row in range(LATE):
-        at = 6 - LATE + row
-        sample(table_ref, 0, 1, arr_ref[at, 9].astype(jnp.int32), [arr_ref[at, d] for d in range(3)], basis_ref.at[row], keeper(row))
     ax, gap = lax.axis_index("ax"), lax.axis_index("gap")
     absent = [ax == 0, ax == sizes[0] - 1, None, None, gap == 0, gap == sizes[2] - 1]
 
@@ -145,27 +146,43 @@
         radial = vel[2] * (1.0 - 0.4)
         return [xi[0] + 0.25 * axial, xi[1] + 0.25 * circ, xi[2] + 1.0 * radial, axial, circ, radial]
 
+    for load in loads[0:5]:
+        load.wait()
     stay = 1.0 - dep_ref[...]
     state = update([xi_ref[d] for d in range(3)], [vel_ref[d] for d in range(3)], fluid_ref[0:64]) + [mom_ref[d] for d in range(3)]
     for at, value in enumerate(state):
         kept_ref[at] = value * stay
+    saves[1].start()
+    for load in loads[5:]:
+        load.wait()
+    saves[0].start()
+    make_table(table_ref, 0, w_ref[...], bary_ref[...])
+    for row in range(LATE):
+        at = 6 - LATE + row
+        sample(table_ref, 0, 1, arr_ref[at, 9].astype(jnp.int32), [arr_ref[at, d] for d in range(3)], basis_ref.at[row], keeper(row))
     for row in range(6):
         state = [arr_ref[row, d] for d in range(11)]
         live = state[10] if absent[row] is None else state[10] * jnp.where(absent[row], 0.0, 1.0)
         fluid = fluid_ref[64 + 8 * row:72 + 8 * row] if row < 6 - LATE else late_ref[row - 6 + LATE]
         for at, value in enumerate(update(state[0:3], state[3:6], fluid) + state[6:9]):
             arrived_ref[row, at] = value * live
+    saves[2].start()
+    for save in saves:
+        save.wait()
 
 def finish(sizes, w, bary, fluid, xi, vel, mom, dep, arr):
+    args = (fluid, vel, xi, mom, dep, w, bary, arr)
+    outs = (jax.ShapeDtypeStruct((256, 128), jnp.float32), jax.ShapeDtypeStruct((9, 64, 128), jnp.float32), jax.ShapeDtypeStruct((6, 9, 8, 128), jnp.float32))
     return pl.pallas_call(
         functools.partial(finish_kernel, sizes),
-        out_shape=(jax.ShapeDtypeStruct((256, 128), jnp.float32), jax.ShapeDtypeStruct((9, 64, 128), jnp.float32), jax.ShapeDtypeStruct((6, 9, 8, 128), jnp.float32)),
-        in_specs=[pl.BlockSpec(memory_space=pltpu.VMEM)] * 8,
-        out_specs=(pl.BlockSpec(memory_space=pltpu.VMEM),) * 3,
-        scratch_shapes=[pltpu.VMEM((1, 128, 768), jnp.bfloat16), pltpu.VMEM((LATE, 4, 64, 128), jnp.float32), pltpu.VMEM((LATE, 8, 128), jnp.float32)],
+        out_shape=outs,
+        in_specs=[pl.BlockSpec(memory_space=pl.ANY)] * 8,
+        out_specs=(pl.BlockSpec(memory_space=pl.ANY),) * 3,
+        scratch_shapes=[pltpu.VMEM(t.shape, t.dtype) for t in args + outs[1:]]
+        + [pltpu.VMEM((1, 128, 768), jnp.bfloat16), pltpu.VMEM((LATE, 4, 64, 128), jnp.float32), pltpu.VMEM((LATE, 8, 128), jnp.float32),
+           pltpu.SemaphoreType.DMA((8,)), pltpu.SemaphoreType.DMA((3,))],
         name="finish",
-    )(w, bary, fluid, xi, vel, mom, dep, arr)
-
+    )(*args)
 
 def diff_table():
     b = bary_weights()

time: 49 us -> 49 us (level)
  no operation moved by 1% of the time
where the time goes in v7:
time: 49 us; the launch traced here: 48.8 us
  Pallas kernels  48.2 us (98%)
  between operations  0.64 us (1%)
    pallas_call x1, Pallas kernels, flow(): pl.pallas_call(functools.partial(flow_kernel, sizes), out_shape=(jax.Shap...  45.5 us
    pallas_call x1, Pallas kernels, finish(): pl.pallas_call(functools.partial(finish_kernel, sizes), out_shape=outs, i...  2.68 us

profile of v7, /device:TPU:1, one launch (start us, length us, event | category | flops | bytes accessed | tf_op | source)
XLA Modules:
  0.0 48.8 jit_solution(11659440156864632532)
XLA Ops:
  0.6 45.5 %flow.1 = (f32[256,128]{1,0:T(8,128)}, f32[6,11,8,128]{3,2,1,0:T(8,128)}, f32[64,128]{1,0:T(8,128)}, f32[96,128]{1,0:T(8,128)}) custom-call(f32[6,32,128]{2,1,0:T(8,128)} %constant.16.clone.refs_0_, f32[256,128]{1,0:T(8,128)} %bitcast.19, f32[256,128]{1,0:T(8,128)} %bitcast.20, bf16[8,384]{1,0:T(8,128)(2,1)} %constant.17.clone.refs_3_, f32[256,128]{1,0:T(8,128)} %bitcast.21, ...), custom_call_target="tpu_custom_call" | custom-call | tf_op jit(solution)/shard_map/flow/pallas_call | solution.py:552
  46.2 2.7 %finish.1 = (f32[256,128]{1,0:T(8,128)}, f32[9,64,128]{2,1,0:T(8,128)}, f32[6,9,8,128]{3,2,1,0:T(8,128)}) custom-call(f32[96,128]{1,0:T(8,128)} %get-tuple-element.10.refs_0_, f32[3,64,128]{2,1,0:T(8,128)} %bitcast.16, f32[3,64,128]{2,1,0:T(8,128)} %bitcast.14, f32[3,64,128]{2,1,0:T(8,128)} %bitcast.18, f32[64,128]{1,0:T(8,128)} %get-tuple-element.11.refs_4_, ...), custom_call_target="tpu_custom_call" | custom-call | tf_op jit(solution)/shard_map/finish/pallas_call | solution.py:176
